TPU v7x, 32 devices: a whole 2x2x4 slice. The times are simulated.
32 devices in a mesh: tm: 8 (over z, y), obs: 4 (over x, core).
Axes of the slice: x: 2, y: 2, z: 4, core: 2. Of those that a mesh axis runs over, the one named last changes fastest.
Arguments:
- obs_rows: float32 [256, 768], P(('tm', 'obs')), may hold values from -6 to 6
- obs_owner: int32 [256, 1], P(('tm', 'obs')), may hold values from 0 to 7; in each aligned block of 8 rows (0 to 7, 8 to 15, ...) at most 2 rows name the same one
- obs_member: int32 [256, 1], P(('tm', 'obs')), may hold values from 0 to 7
- prior_diag: float32 [64, 384], P(('tm', 'obs')), may hold values from 1 to 4
- lower_coupling: float32 [64, 384, 384], P(('tm', 'obs')), may hold values from -2 to 2
- tip_coupling: float32 [64, 128, 384], P(('tm', 'obs')), may hold values from -0.095683193 to 0.095683193
- time_rhs: float32 [64, 384], P(('tm', 'obs')), may hold values from -6 to 6
- tip_prior: float32 [128], replicated, may hold values from 0.5 to 2
- tip_rhs: float32 [128], replicated, may hold values from -30 to 30
Outputs:
- reduced_block: float32 [64, 384, 384], P(('tm', 'obs'))
- reduced_lower: float32 [64, 384, 384], P(('tm', 'obs'))
- reduced_tip: float32 [64, 128, 384], P(('tm', 'obs'))
- time_result: float32 [64, 384], P(('tm', 'obs'))
- tip_solution: float32 [128], replicated
Inputs may be any that keep to these rules, and one draw needn't show every extreme that they name: `obs_owner`: of the 8 observation blocks of one device, at most 2 name the same owner group, and in every draw some device has an owner group named exactly 2 times.
All inputs are finite; a program needn't handle non-finite values.
Results may differ from a plain program's by a relative error of at most 0.00016.
Values sent between devices are 32-bit elements; how exact they have to be, the bound alone decides.
A program may use at most 64 MiB of HBM per device.

v0:
```python
import jax
import jax.numpy as jnp
from jax import lax
from jax.sharding import PartitionSpec as P

R = 2
CAP = 2


FULL_PRECISION = lax.Precision.HIGHEST


def shifted(value, axis, steps):
    count = lax.axis_size(axis)
    first, last = (max(0, -steps), min(count, count - steps))
    return lax.ppermute(value, axis, [(source, source + steps) for source in range(first, last)])


def lower_solve(factor, right, transpose=False):
    return lax.linalg.triangular_solve(
        factor, right, left_side=True, lower=True, transpose_a=transpose
    )


def cross_product(left, right):
    return lax.dot_general(
        left,
        right,
        (((0,), (0,)), ((), ())),
        precision=FULL_PRECISION,
        preferred_element_type=jnp.float32,
    )


def masked_gram(flat_rows, chosen_mask):
    chosen = flat_rows * chosen_mask[:, None]
    return cross_product(chosen, flat_rows)


def local(
    obs_rows,
    obs_owner,
    obs_member,
    prior_diag,
    lower_coupling,
    tip_coupling,
    time_rhs,
    tip_prior,
    tip_rhs,
):
    groups = lax.axis_size("tm")
    position = lax.axis_index(("tm", "obs"))
    member_index = lax.axis_index("obs")
    block_width = prior_diag.shape[1]
    blocks = obs_rows.shape[0]
    owners = obs_owner[:, 0]
    ordinal = jnp.arange(blocks, dtype=jnp.int32)
    earlier = (owners[:, None] == owners[None, :]) & (ordinal[None, :] < ordinal[:, None])
    slot_rank = jnp.sum(earlier.astype(jnp.int32), axis=1)
    slot_index = owners * CAP + slot_rank
    outgoing = (
        jnp.zeros((groups * CAP, obs_rows.shape[1]), jnp.float32).at[slot_index].set(obs_rows)
    )
    labels = (
        jnp.full((groups * CAP,), -1.0, jnp.float32)
        .at[slot_index]
        .set(obs_member[:, 0].astype(jnp.float32))
    )
    outgoing = outgoing.reshape(groups, CAP, obs_rows.shape[1])
    labels = labels.reshape(groups, CAP)
    arrived, arrived_tags = (
        lax.all_to_all(outgoing, "tm", split_axis=0, concat_axis=0, tiled=True),
        lax.all_to_all(labels, "tm", split_axis=0, concat_axis=0, tiled=True),
    )
    even_member = (2 * member_index).astype(jnp.float32)
    rows_part = lax.all_gather(arrived, "obs", axis=0, tiled=True)
    tag_part = lax.all_gather(arrived_tags, "obs", axis=0, tiled=True)
    rows_flat = rows_part.reshape(-1, block_width)
    tag_flat = jnp.broadcast_to(tag_part.reshape(-1, 1), (tag_part.size, R)).reshape(-1)
    even_gram = masked_gram(rows_flat, (tag_flat == even_member).astype(jnp.float32))
    odd_gram = masked_gram(rows_flat, (tag_flat == even_member + 1.0).astype(jnp.float32))
    own_gram = jnp.stack([even_gram, odd_gram], axis=0)
    identity = jnp.eye(block_width, dtype=jnp.float32)
    own_blocks = own_gram + prior_diag[:, :, None] * identity
    even_lower = jnp.where(position == 0, jnp.zeros_like(lower_coupling[0]), lower_coupling[0])
    odd_lower = lower_coupling[1]
    even_tip = tip_coupling[0]
    odd_tip = tip_coupling[1]
    factor = jnp.linalg.cholesky(own_blocks[0])
    stacked = jnp.concatenate([even_lower, even_tip.T, time_rhs[0][:, None], odd_lower.T], axis=1)
    solved = lower_solve(factor, stacked)
    tip_width = even_tip.shape[0]
    fill_block = solved[:, :block_width]
    tip_side = solved[:, block_width : block_width + tip_width]
    lifted = solved[:, block_width + tip_width]
    left_cross = solved[:, block_width + tip_width + 1 :]
    tip_terms = (
        cross_product(even_tip.T, even_tip.T)
        + cross_product(odd_tip.T, odd_tip.T)
        - cross_product(tip_side, tip_side)
    )
    tip_lift = cross_product(tip_side, lifted)
    schur_sum, lift_sum = lax.psum((tip_terms, tip_lift), ("tm", "obs"))
    right_fill, right_side, right_lift = shifted((fill_block, tip_side, lifted), ("tm", "obs"), -1)
    schur_block = schur_sum + jnp.diag(tip_prior)
    chol_tip = jnp.linalg.cholesky(schur_block)
    halfway = lower_solve(chol_tip, (tip_rhs - lift_sum)[:, None])
    tip_solution = lower_solve(chol_tip, halfway, True)[:, 0]
    pulled = lifted - jnp.dot(tip_side, tip_solution, precision=FULL_PRECISION)
    estimate = lower_solve(factor, pulled[:, None], True)[:, 0]
    new_block = (
        own_blocks[1]
        - cross_product(left_cross, left_cross)
        - cross_product(right_fill, right_fill)
    )
    new_lower = -cross_product(left_cross, fill_block)
    new_tip = odd_tip - cross_product(tip_side, left_cross) - cross_product(right_side, right_fill)
    new_rhs = (
        time_rhs[1] - cross_product(left_cross, lifted) - cross_product(right_fill, right_lift)
    )
    reduced_block = jnp.stack([factor, new_block], axis=0)
    reduced_lower = jnp.stack([fill_block, new_lower], axis=0)
    reduced_tip = jnp.stack([tip_side.T, new_tip], axis=0)
    time_result = jnp.stack([estimate, new_rhs], axis=0)
    return (reduced_block, reduced_lower, reduced_tip, time_result, tip_solution)


def solution(mesh):
    in_specs = (
        P(("tm", "obs"), None),
        P(("tm", "obs"), None),
        P(("tm", "obs"), None),
        P(("tm", "obs"), None),
        P(("tm", "obs"), None, None),
        P(("tm", "obs"), None, None),
        P(("tm", "obs"), None),
        P(),
        P(),
    )
    out_specs = (
        P(("tm", "obs"), None, None),
        P(("tm", "obs"), None, None),
        P(("tm", "obs"), None, None),
        P(("tm", "obs"), None),
        P(),
    )
    return jax.shard_map(local, mesh=mesh, in_specs=in_specs, out_specs=out_specs, check_vma=False)
```

profile of v0, /device:TPU:1, one launch (start us, length us, event | category | flops | bytes accessed | tf_op | source)
XLA Modules:
  0.0 350.8 jit_solution(14849988606547556915)
XLA Ops:
  7.2 1.0 convert_reduce_fusion
  10.1 6.4 %all-to-all-start.1 = ((f32[8,1,2]{2,1,0:T(1,128)}), f32[8,1,2]{2,1,0:T(1,128)S(1)}, u32[]{:S(2)}, u32[]{:S(2)}) async-start(f32[8,1,2]{2,1,0:T(1,128)} %bitcast.4), calls=%async_computation.1 | async-start | bytes 8192 | tf_op jit(solution)/shard_map/all_to_all | solution.py:73
  17.1 1.4 fusion.21
  18.5 1.6 slice_bitcast_fusion.3
  20.1 1.9 slice_reduce_fusion
  23.5 1.0 convolution_add_fusion
  24.9 1.0 pad_maximum_fusion
  26.0 5.4 %all-to-all-start = ((f32[8,2,768]{2,1,0:T(2,128)}), f32[8,2,768]{2,1,0:T(2,128)S(1)}, u32[]{:S(2)}, u32[]{:S(2)}) async-start(f32[8,2,768]{2,1,0:T(2,128)} %reshape.135), calls=%async_computation | async-start | bytes 98304 | tf_op jit(solution)/shard_map/all_to_all | solution.py:72
  31.5 6.6 %all-gather = f32[32,1,2]{2,1,0:T(1,128)S(1)} all-gather(f32[8,1,2]{2,1,0:T(1,128)S(1)} %all-to-all-done.1), channel_id=2, replica_groups=mesh['tm'=8,'obs'=4] {'obs'}, dimensions={0}, use_global_device_ids=true | all-gather | bytes 320 | tf_op jit(solution)/shard_map/all_gather | solution.py:77
  38.3 7.2 %all_gather.6 = f32[32,2,768]{2,1,0:T(2,128)S(1)} all-gather(f32[8,2,768]{2,1,0:T(2,128)S(1)} %all-to-all-done), channel_id=1, replica_groups=mesh['tm'=8,'obs'=4] {'obs'}, dimensions={0}, use_global_device_ids=true | all-gather | bytes 245760 | tf_op jit(solution)/shard_map/all_gather | solution.py:76
  48.5 1.3 copy.124
  50.6 11.7 %cholesky.101 = f32[128,128]{1,0:T(8,128)S(1)} custom-call(f32[128,128]{1,0:T(8,128)S(1)} %cholesky.248), custom_call_target="Cholesky" | custom-call | tf_op jit(solution)/shard_map/jit(cholesky)/cholesky | solution.py:89
  63.1 9.8 %custom-call.32 = f32[1,128,128]{1,2,0:T(8,128)S(1)} custom-call(f32[1,128,128]{2,1,0:T(8,128)S(1)} %get-tuple-element.90), custom_call_target="InvertDiagBlocksLowerTriangular" | custom-call | tf_op jit(solution)/shard_map/jit(cholesky)/cholesky | solution.py:89
  72.9 1.2 fusion.28
  74.1 1.2 convolution_subtract_fusion.6
  76.1 12.2 %cholesky.209 = f32[128,128]{1,0:T(8,128)S(1)} custom-call(f32[128,128]{1,0:T(8,128)S(1)} %cholesky.252), custom_call_target="Cholesky" | custom-call | tf_op jit(solution)/shard_map/jit(cholesky)/cholesky | solution.py:89
  89.5 10.4 %custom-call.33 = f32[1,128,128]{1,2,0:T(8,128)} custom-call(f32[1,128,128]{2,1,0:T(8,128)S(1)} %get-tuple-element.88), custom_call_target="InvertDiagBlocksLowerTriangular" | custom-call | tf_op jit(solution)/shard_map/jit(cholesky)/cholesky | solution.py:89
  102.6 1.2 convolution_dynamic-update-slice_fusion
  103.8 1.9 convolution_subtract_fusion.7
  105.7 13.2 %cholesky.228 = f32[128,128]{1,0:T(8,128)} custom-call(f32[128,128]{1,0:T(8,128)} %convolution_subtract_fusion.7), custom_call_target="Cholesky" | custom-call | tf_op jit(solution)/shard_map/jit(cholesky)/cholesky | solution.py:89
  118.8 1.4 select_reduce_fusion.1
  120.3 1.6 copy.129
  122.5 1.2 compare_reduce_fusion.2
  123.7 1.3 compare_reduce_fusion.1
  127.8 1.1 fusion.13
  129.6 11.0 %while.1 = (s32[]{:T(128)}, f32[384,384]{0,1:T(8,128)}, s32[3,2]{0,1:T(2,128)S(1)}, f32[3,128,128]{2,1,0:T(8,128)}, s32[]{:T(128)}) while((s32[]{:T(128)}, f32[384,384]{0,1:T(8,128)}, s32[3,2]{0,1:T(2,128)S(1)}, f32[3,128,128]{2,1,0:T(8,128)}, s32[]{:T(128)}) %tuple.45), condition=%wide.while_cond, body=%wide.while_body.sunk | while | flops 2 | bytes 393329 | solution.py:20
  130.4 2.3 dynamic-slice.7
  134.1 2.3 dynamic-slice.7
  137.7 2.2 dynamic-slice.7
  140.6 30.3 %custom-call.34 = f32[3,128,128]{1,2,0:T(8,128)S(1)} custom-call(f32[3,128,128]{2,1,0:T(8,128)} %get-tuple-element.12), custom_call_target="InvertDiagBlocksLowerTriangular" | custom-call | tf_op jit(solution)/shard_map/triangular_solve | solution.py:20
  172.5 1.8 convolution_subtract_fusion.3
  177.2 2.1 convolution_subtract_fusion.1
  180.3 1.5 convolution_subtract_fusion.5
  181.8 2.2 collective-permute-start.1
  184.0 1.3 fusion.1
  186.2 1.9 collective-permute-start.2
  188.1 1.0 convolution_subtract_fusion.8
  189.3 1.4 copy.137
  190.7 2.3 collective-permute-start
  192.9 43.8 %psum.15 = f32[128]{0:T(128)S(1)} all-reduce(f32[128]{0:T(128)S(1)} %convolution_bitcast_fusion.8), channel_id=1, replica_groups=mesh['tm'=8,'obs'=4] {'tm','obs'}, use_global_device_ids=true, to_apply=%region_12.13 | all-reduce | flops 128 | bytes 1024 | tf_op jit(solution)/shard_map/psum | solution.py:103
  236.7 73.9 %all-reduce.3.cloned.1.call-done = f32[128,128]{1,0:T(8,128)} async-done(((f32[128,128]{1,0:T(8,128)}), f32[128,128]{1,0:T(8,128)}) %all-reduce.3.cloned.1.call-update) | async-done | bytes 65552 | tf_op jit(solution)/shard_map/psum | solution.py:103
  310.6 0.9 select_add_fusion
  311.6 0.9 fusion.38
  312.6 11.7 %cholesky.240 = f32[128,128]{1,0:T(8,128)S(1)} custom-call(f32[128,128]{1,0:T(8,128)S(1)} %fusion.38), custom_call_target="Cholesky" | custom-call | tf_op jit(solution)/shard_map/jit(cholesky)/cholesky | solution.py:106
  325.6 9.8 %custom-call.35 = f32[1,128,128]{1,2,0:T(8,128)S(1)} custom-call(f32[1,128,128]{2,1,0:T(8,128)S(1)} %fusion.30), custom_call_target="InvertDiagBlocksLowerTriangular" | custom-call | tf_op jit(solution)/shard_map/triangular_solve | solution.py:20
  338.0 1.3 fusion
  339.4 1.4 copy.136
  340.8 1.6 fusion.2
  (122 shorter events, 31.9 us)
Async XLA Ops:
  7.2 16.4 %copy-start.4 = (f32[2,128,384]{2,1,0:T(8,128)S(1)}, f32[2,128,384]{2,1,0:T(8,128)}, u32[]{:S(2)}) copy-start(f32[2,128,384]{2,1,0:T(8,128)} %param.14) | copy-start | bytes 1179652
  7.2 17.4 %copy-start.5 = (f32[2,384,384]{2,1,0:T(8,128)S(1)}, f32[2,384,384]{2,1,0:T(8,128)}, u32[]{:S(2)}) copy-start(f32[2,384,384]{2,1,0:T(8,128)} %param.13) | copy-start | bytes 3538948
  10.1 15.8 %all-to-all-start.1 = ((f32[8,1,2]{2,1,0:T(1,128)}), f32[8,1,2]{2,1,0:T(1,128)S(1)}, u32[]{:S(2)}, u32[]{:S(2)}) async-start(f32[8,1,2]{2,1,0:T(1,128)} %bitcast.4), calls=%async_computation.1 | async-start | bytes 8192 | tf_op jit(solution)/shard_map/all_to_all | solution.py:73
  26.0 12.3 %all-to-all-start = ((f32[8,2,768]{2,1,0:T(2,128)}), f32[8,2,768]{2,1,0:T(2,128)S(1)}, u32[]{:S(2)}, u32[]{:S(2)}) async-start(f32[8,2,768]{2,1,0:T(2,128)} %reshape.135), calls=%async_computation | async-start | bytes 98304 | tf_op jit(solution)/shard_map/all_to_all | solution.py:72
  31.4 279.2 %all-reduce.3.cloned.1.call-start = ((), (), s32[]{:S(2)}) async-start(), calls=%async_computation.2 | async-start | bytes 131072 | tf_op jit(solution)/shard_map/psum | solution.py:103
  45.8 1.7 copy-start.13
  49.8 0.8 copy-start.3
  75.3 14.3 %copy-start.10 = (f32[256,128]{1,0:T(8,128)}, f32[256,128]{1,0:T(8,128)S(1)}, u32[]{:S(2)}) copy-start(f32[256,128]{1,0:T(8,128)S(1)} %convolution_subtract_fusion.6) | copy-start | bytes 393220
  170.9 0.7 copy-start.7
  172.5 1.8 copy-start.8
  172.5 2.7 copy-start
  181.8 6.3 %copy-start.11 = (f32[128,128]{1,0:T(8,128)S(1)}, f32[128,128]{1,0:T(8,128)}, u32[]{:S(2)}) copy-start(f32[128,128]{1,0:T(8,128)} %convolution_add_fusion) | copy-start | bytes 196612
  181.8 159.0 %collective-permute-start.1 = (f32[384,128]{0,1:T(8,128)S(1)}, f32[384,128]{0,1:T(8,128)}, u32[]{:S(2)}, u32[]{:S(2)}) collective-permute-start(f32[384,128]{0,1:T(8,128)S(1)} %pad_maximum_fusion.5), channel_id=1, source_target_pairs={{1,0},{2,1},{3,2},{4,3},{5,4},{6,5},{7,6},{8,7},{9,8},{10,9},{11,1... | collective-permute-start | bytes 589832 | tf_op jit(solution)/shard_map/ppermute | solution.py:16
  186.2 50.5 %collective-permute-start.2 = (f32[384]{0:T(512)S(1)}, f32[384]{0:T(512)S(1)}, u32[]{:S(2)}, u32[]{:S(2)}) collective-permute-start(f32[384]{0:T(512)S(1)} %get-tuple-element.75), channel_id=1, source_target_pairs={{1,0},{2,1},{3,2},{4,3},{5,4},{6,5},{7,6},{8,7},{9,8},{10,9},{11,1... | collective-permute-start | bytes 4616 | tf_op jit(solution)/shard_map/ppermute | solution.py:16
  189.2 121.4 %copy-start.14 = (f32[128]{0:T(128)S(1)}, f32[128]{0:T(128)}, u32[]{:S(2)}) copy-start(f32[128]{0:T(128)} %param.16) | copy-start | bytes 1540
  189.2 146.2 %copy-start.16 = (f32[128]{0:T(128)S(1)}, f32[128]{0:T(128)}, u32[]{:S(2)}) copy-start(f32[128]{0:T(128)} %param.17) | copy-start | bytes 1540
  189.2 146.9 %copy-start.9 = (f32[3,128,128]{1,2,0:T(8,128)S(1)}, f32[3,128,128]{1,2,0:T(8,128)}, u32[]{:S(2)}) copy-start(f32[3,128,128]{1,2,0:T(8,128)} %copy-done.7) | copy-start | bytes 589828
  190.6 147.3 %copy-start.12 = (f32[384]{0:T(512)S(1)}, f32[384]{0:T(512)}, u32[]{:S(2)}) copy-start(f32[384]{0:T(512)} %get-tuple-element.91) | copy-start | bytes 4612
  190.6 147.3 %copy-start.1 = (f32[384,384]{0,1:T(8,128)S(1)}, f32[384,384]{0,1:T(8,128)}, u32[]{:S(2)}) copy-start(f32[384,384]{0,1:T(8,128)} %convolution_subtract_fusion.1) | copy-start | bytes 1769476
  190.7 146.6 %collective-permute-start = (f32[384,384]{0,1:T(8,128)}, f32[384,384]{0,1:T(8,128)S(1)}, u32[]{:S(2)}, u32[]{:S(2)}) collective-permute-start(f32[384,384]{0,1:T(8,128)} %get-tuple-element.80), channel_id=1, source_target_pairs={{1,0},{2,1},{3,2},{4,3},{5,4},{6,5},{7,6},{8,7},{9,8},{10,9},{11,1... | collective-permute-start | bytes 1769480 | tf_op jit(solution)/shard_map/ppermute | solution.py:16
  335.8 3.4 copy-start.15
  337.2 2.0 copy-start.2
  339.4 1.4 copy-start.6
Sparse Core Ops, SparseCore 0:
  189.3 121.3 all-reduce.2
where the time goes:
time: 355 us; the launch traced here: 351 us
  other arithmetic  124 us (35%)
  waiting for transfers between devices  73.9 us (21%)
  blocking collectives  57.5 us (16%)
  local copies, waits for them, and re-layouts  33.6 us (9%)
  matrix products  26.6 us (7%)
  starting transfers between devices  18.2 us (5%)
  between operations  16.8 us (5%)
    psum x1, waiting for transfers between devices, local(): schur_sum, lift_sum = lax.psum((tip_terms, tip_lift), ('tm', 'obs'))  73.9 us
    another operation x11, other arithmetic, local(): factor = jnp.linalg.cholesky(own_blocks[0])  62.6 us
    psum x1, blocking collectives, local(): schur_sum, lift_sum = lax.psum((tip_terms, tip_lift), ('tm', 'obs'))  43.8 us
    another operation x5, other arithmetic, lower_solve(): lax.linalg.triangular_solve(factor, right, left_side=True, lower=True, tr...  41.5 us
    dot_general x13, matrix products, cross_product(): lax.dot_general(left, right, (((0,), (0,)), ((), ())), precision=FULL_PRE...  14.2 us
    another operation x3, other arithmetic, local(): chol_tip = jnp.linalg.cholesky(schur_block)  12.4 us
    another operation x15, local copies, waits for them, and re-layouts  10.8 us
    another operation x10, local copies, waits for them, and re-layouts, local(): factor = jnp.linalg.cholesky(own_blocks[0])  7.26 us
  transfers between devices with their start and end apart: 6, of which 1 were waited for; matrix products, arithmetic and copies ran while one was open for 13% of the time, Pallas kernels for 0%

commit v1 on v0

v1 whole, which is shorter than its diff:
```python
import jax
import jax.numpy as jnp
from jax import lax
from jax.experimental import pallas as pl
from jax.experimental.pallas import tpu as pltpu
from jax.sharding import PartitionSpec as P

R = 2
CAP = 2
T = 128
PANEL = 8
HI = lax.Precision.HIGHEST
VMEM = pl.BlockSpec(memory_space=pltpu.VMEM)


def dot_nn(a, b):
    return lax.dot_general(a, b, (((1,), (0,)), ((), ())), precision=HI, preferred_element_type=jnp.float32)


def dot_nt(a, b):
    return lax.dot_general(a, b, (((1,), (1,)), ((), ())), precision=HI, preferred_element_type=jnp.float32)


def dot_tn(a, b):
    return lax.dot_general(a, b, (((0,), (0,)), ((), ())), precision=HI, preferred_element_type=jnp.float32)


def split3(x):
    h = x.astype(jnp.bfloat16).astype(jnp.float32)
    rest = x - h
    m = rest.astype(jnp.bfloat16).astype(jnp.float32)
    return h, m, rest - m


def panel_gram(rows):
    h, m, l = split3(rows)
    left = jnp.concatenate([part[:, :T] for part in (h, h, m, h, l, m)], axis=0)
    right = jnp.concatenate([h, m, h, l, h, m], axis=0)
    return lax.dot_general(
        left.astype(jnp.bfloat16),
        right.astype(jnp.bfloat16),
        (((0,), (0,)), ((), ())),
        preferred_element_type=jnp.float32,
    )


def factor_tile(work):
    sub = lax.broadcasted_iota(jnp.int32, (PANEL, 2 * T), 0)
    sub_t = lax.broadcasted_iota(jnp.int32, (PANEL, T), 0)
    for p in range(T // PANEL):
        base = p * PANEL
        rows = work[base : base + PANEL, :]
        cols = [
            jnp.broadcast_to(rows[:, base + j : base + j + 1], (PANEL, T)) for j in range(PANEL)
        ]
        scale = jnp.zeros((PANEL, T), jnp.float32)
        for i in range(PANEL):
            pivot = jnp.broadcast_to(cols[i][i : i + 1, :], (PANEL, T))
            root = lax.rsqrt(pivot)
            root = root * (1.5 - 0.5 * pivot * root * root)
            scale = jnp.where(sub_t == i, root, scale)
            if i + 1 < PANEL:
                mult = jnp.where(sub_t > i, cols[i] * (root * root), 0.0)
                mult2 = jnp.concatenate([mult, mult], axis=1)
                rows = rows - mult2 * jnp.broadcast_to(rows[i : i + 1, :], (PANEL, 2 * T))
                for j in range(i + 1, PANEL):
                    cols[j] = cols[j] - mult * jnp.broadcast_to(cols[j][i : i + 1, :], (PANEL, T))
        rows = rows * jnp.concatenate([scale, scale], axis=1)
        work[base : base + PANEL, :] = rows
        if base + PANEL < T:
            work[base + PANEL :, :] = work[base + PANEL :, :] - panel_gram(rows)[base + PANEL :, :]


def eye(n):
    return (
        lax.broadcasted_iota(jnp.int32, (n, n), 0) == lax.broadcasted_iota(jnp.int32, (n, n), 1)
    ).astype(jnp.float32)


def upper_mask(n):
    return lax.broadcasted_iota(jnp.int32, (n, n), 0) <= lax.broadcasted_iota(jnp.int32, (n, n), 1)


def local_kernel(
    rows_ref, tag_ref, label_ref, prior_ref, lower_ref, tip_ref, rhs_ref,
    factor_ref, fill_ref, newlow_ref, side_ref, lift_ref, partblk_ref, parttip_ref, partrhs_ref,
    inv_ref, terms_ref, tlift_ref,
    gram, work, y,
):
    B = prior_ref.shape[1]
    K = tip_ref.shape[1]
    nb = B // T
    tags = tag_ref[...]
    even = label_ref[0:1, 0:1]
    rows = rows_ref[...]
    identity = eye(B)
    chosen = jnp.where(tags == even, rows, 0.0)
    gram[...] = dot_tn(chosen, chosen) + prior_ref[0:1, :] * identity
    inv_ref[...] = jnp.zeros((B, B), jnp.float32)
    factor_ref[...] = jnp.zeros((B, B), jnp.float32)
    upper = upper_mask(T)
    for b in range(nb):
        lo, hi = b * T, (b + 1) * T
        work[:, :T] = gram[lo:hi, lo:hi]
        work[:, T:] = eye(T)
        factor_tile(work)
        inv = jnp.where(upper.T, work[:, T:], 0.0)
        factor_ref[lo:hi, lo:hi] = jnp.where(upper, work[:, :T], 0.0).T
        inv_ref[lo:hi, lo:hi] = inv
        if b > 0:
            inv_ref[lo:hi, :lo] = -dot_nn(inv, dot_nn(factor_ref[lo:hi, :lo], inv_ref[:lo, :lo]))
        if b + 1 < nb:
            upper_rest = dot_nn(inv, gram[lo:hi, hi:])
            gram[hi:, hi:] = gram[hi:, hi:] - dot_tn(upper_rest, upper_rest)
            factor_ref[hi:, lo:hi] = upper_rest.T
    linv = inv_ref[...]
    y[:B, :] = lower_ref[1]
    y[B : B + K, :] = tip_ref[0]
    y[B + K :, :] = jnp.concatenate([rhs_ref[0:1, :], jnp.zeros((7, B), jnp.float32)], axis=0)
    y[...] = dot_nt(y[...], linv)
    fill = dot_nn(linv, lower_ref[0])
    fill_ref[...] = fill
    side = y[B : B + K, :]
    side_ref[...] = side
    lift_ref[...] = y[B + K : B + K + 1, :]
    xt = y[:B, :]
    terms_ref[...] = (
        dot_nt(tip_ref[0], tip_ref[0]) + dot_nt(tip_ref[1], tip_ref[1]) - dot_nt(side, side)
    )
    tlift_ref[...] = dot_nt(y[B + K :, :], side)[0:1, :]
    newlow_ref[...] = -dot_nn(xt, fill)
    back = dot_nt(y[...], xt)
    chosen_odd = jnp.where(tags == even + 1.0, rows, 0.0)
    partblk_ref[...] = dot_tn(chosen_odd, chosen_odd) + prior_ref[1:2, :] * identity - back[:B]
    parttip_ref[...] = tip_ref[1] - back[B : B + K]
    partrhs_ref[...] = rhs_ref[1:2, :] - back[B + K : B + K + 1]


def finish_kernel(fill_ref, side_ref, lift_ref, blk_ref, tip_ref, rhs_ref, oblk, otip, orhs):
    fill = fill_ref[...]
    oblk[...] = blk_ref[...] - dot_tn(fill, fill)
    otip[...] = tip_ref[...] - dot_nn(side_ref[...], fill)
    lift = jnp.concatenate([lift_ref[...]] * 8, axis=0)
    orhs[...] = rhs_ref[...] - dot_nn(lift, fill)[0:1, :]


def tip_kernel(schur_ref, prior_ref, crhs_ref, clift_ref, side_ref, lift_ref, inv_ref, sol_ref, est_ref, work):
    work[:, :T] = schur_ref[...] + prior_ref[...] * eye(T)
    work[:, T:] = eye(T)
    factor_tile(work)
    inv = jnp.where(upper_mask(T).T, work[:, T:], 0.0)
    vec = jnp.concatenate([crhs_ref[...] - clift_ref[...]] * 8, axis=0)
    sol = dot_nn(dot_nt(vec, inv), inv)
    sol_ref[...] = sol[0:1, :]
    lift = jnp.concatenate([lift_ref[...]] * 8, axis=0)
    pulled = lift - dot_nn(sol, side_ref[...])
    est_ref[...] = dot_nn(pulled, inv_ref[...])[0:1, :]


def call(kernel, outs, scratch=()):
    return pl.pallas_call(
        kernel,
        out_shape=[jax.ShapeDtypeStruct(s, jnp.float32) for s in outs],
        scratch_shapes=[pltpu.VMEM(s, jnp.float32) for s in scratch],
        compiler_params=pltpu.CompilerParams(vmem_limit_bytes=56 << 20),
    )


def shifted(value, axis, steps):
    count = lax.axis_size(axis)
    first, last = (max(0, -steps), min(count, count - steps))
    return lax.ppermute(value, axis, [(source, source + steps) for source in range(first, last)])


def local(
    obs_rows, obs_owner, obs_member, prior_diag, lower_coupling, tip_coupling, time_rhs, tip_prior, tip_rhs,
):
    groups = lax.axis_size("tm")
    position = lax.axis_index(("tm", "obs"))
    member_index = lax.axis_index("obs")
    B = prior_diag.shape[1]
    K = tip_coupling.shape[1]
    blocks = obs_rows.shape[0]
    owners = obs_owner[:, 0]
    ordinal = jnp.arange(blocks, dtype=jnp.int32)
    earlier = (owners[:, None] == owners[None, :]) & (ordinal[None, :] < ordinal[:, None])
    slot_rank = jnp.sum(earlier.astype(jnp.int32), axis=1)
    slot_index = owners * CAP + slot_rank
    pick = (jnp.arange(groups * CAP, dtype=jnp.int32)[:, None] == slot_index[None, :]).astype(jnp.float32)
    tagged = jnp.concatenate(
        [obs_rows, jnp.broadcast_to(obs_member.astype(jnp.float32) + 1.0, (blocks, 128))], axis=1
    )
    outgoing = jnp.dot(pick, tagged, precision=HI).reshape(groups, CAP, -1)
    arrived = lax.all_to_all(outgoing, "tm", split_axis=0, concat_axis=0, tiled=True)
    gathered = lax.all_gather(arrived, "obs", axis=0, tiled=True)
    rows_part = gathered[:, :, : R * B].reshape(-1, B)
    tags = jnp.broadcast_to(gathered[:, :, R * B :][:, :, None, :1], gathered.shape[:2] + (R, 1)).reshape(-1, 1)
    label = jnp.full((8, 128), 2 * member_index + 1, jnp.float32)
    masked_lower = jnp.where(position == 0, jnp.zeros_like(lower_coupling[0]), lower_coupling[0])
    lower = jnp.stack([masked_lower, lower_coupling[1]])
    (factor, fill, newlow, side, lift, pblk, ptip, prhs, inv, terms, tlift) = call(
        local_kernel,
        [(B, B), (B, B), (B, B), (K, B), (1, B), (B, B), (K, B), (1, B), (B, B), (K, K), (1, K)],
        [(B, B), (T, 2 * T), (B + K + 8, B)],
    )(rows_part, tags, label, prior_diag, lower, tip_coupling, time_rhs)
    nfill, nside, nlift = shifted((fill, side, lift), ("tm", "obs"), -1)
    schur, slift = lax.psum((terms, tlift), ("tm", "obs"))
    sol, est = call(tip_kernel, [(1, K), (1, B)], [(T, 2 * T)])(
        schur, tip_prior[None, :], tip_rhs[None, :], slift, side, lift, inv
    )
    nblk, ntip, nrhs = call(finish_kernel, [(B, B), (K, B), (1, B)])(nfill, nside, nlift, pblk, ptip, prhs)
    return (
        jnp.stack([factor, nblk]),
        jnp.stack([fill, newlow]),
        jnp.stack([side, ntip]),
        jnp.concatenate([est, nrhs], axis=0),
        sol[0],
    )


def solution(mesh):
    split = ("tm", "obs")
    two, three = P(split, None), P(split, None, None)
    return jax.shard_map(
        local,
        mesh=mesh,
        in_specs=(two, two, two, two, three, three, two, P(), P()),
        out_specs=(three, three, three, two, P()),
        check_vma=False,
    )
```

time: 355 us -> 213 us (0.60); the launches traced: 351 us -> 213 us
  other arithmetic: 124 us -> 10.5 us
  Pallas kernels: 0 us -> 44.6 us
  local copies, waits for them, and re-layouts: 33.6 us -> 4.07 us
  matrix products: 26.6 us -> 0.89 us
  blocking collectives: 57.5 us -> 47.7 us
  starting transfers between devices: 18.2 us -> 12.3 us
  waiting for transfers between devices: 73.9 us -> 78.5 us
    another operation x25 -> x4, other arithmetic: 119 us -> 6.4 us  [the longest x1 2.34 us: local(): jnp.stack([fill, newlow])]
    pallas_call x0 -> x3, Pallas kernels: none -> 44.6 us  [the longest x1 31.4 us: local(): call(local_kernel, [(B, B), (B, B), (B, B), (K, B), (1, B), (B, B), (K, B...]
    another operation x28 -> x0, local copies, waits for them, and re-layouts: 19.7 us -> none
    dot_general x14 -> x1, matrix products: 14.5 us -> 0.89 us  [local(): outgoing = jnp.dot(pick, tagged, precision=HI).reshape(groups, CAP, -1)]
    another operation x16 -> x0, matrix products: 12.1 us -> none  [the longest x12 6.74 us: lower_solve(): lax.linalg.triangular_solve(factor, right, left_side=True, lower=True, tr...]
    all_to_all x1 -> x0, starting transfers between devices: 6.37 us -> none  [local(): lax.all_to_all(labels, 'tm', split_axis=0, concat_axis=0, tiled=True)]
    all_gather x2 -> x1, blocking collectives: 13.7 us -> 7.61 us  [local(): gathered = lax.all_gather(arrived, 'obs', axis=0, tiled=True)]
    psum x1, blocking collectives: 43.8 us -> 40.1 us  [local(): schur, slift = lax.psum((terms, tlift), ('tm', 'obs'))]
  transfers between devices with their start and end apart: 6 -> 5, of which waited for: 1 -> 2; matrix products, arithmetic and copies ran while one was open for 13% -> 2% of each run, Pallas kernels for 0% -> 4%
where the time goes in v1:
time: 213 us
  waiting for transfers between devices  78.5 us (37%)
  blocking collectives  47.7 us (22%)
  Pallas kernels  44.6 us (21%)
  between operations  14.2 us (7%)
  starting transfers between devices  12.3 us (6%)
  other arithmetic  10.5 us (5%)
  local copies, waits for them, and re-layouts  4.07 us (2%)
    psum x1, waiting for transfers between devices, local(): schur, slift = lax.psum((terms, tlift), ('tm', 'obs'))  75.2 us
    psum x1, blocking collectives, local(): schur, slift = lax.psum((terms, tlift), ('tm', 'obs'))  40.1 us
    pallas_call x1, Pallas kernels, local(): call(local_kernel, [(B, B), (B, B), (B, B), (K, B), (1, B), (B, B), (K, B...  31.4 us
    pallas_call x1, Pallas kernels, local(): call(tip_kernel, [(1, K), (1, B)], [(T, 2 * T)])  9.42 us
    all_gather x1, blocking collectives, local(): gathered = lax.all_gather(arrived, 'obs', axis=0, tiled=True)  7.61 us
    all_to_all x1, starting transfers between devices, local(): lax.all_to_all(outgoing, 'tm', split_axis=0, concat_axis=0, tiled=True)  6.37 us
    ppermute x3, starting transfers between devices, shifted(): lax.ppermute(value, axis, [(source, source + steps) for source in range(f...  5.9 us
  transfers between devices with their start and end apart: 5, of which 2 were waited for; matrix products, arithmetic and copies ran while one was open for 2% of the time, Pallas kernels for 4%

profile of v1, /device:TPU:1, one launch (start us, length us, event | category | flops | bytes accessed | tf_op | source)
XLA Modules:
  0.0 212.7 jit_solution(8442362268561912432)
XLA Ops:
  7.2 0.7 add_bitcast_fusion
  7.8 0.9 convert_reduce_fusion
  8.7 0.7 multiply_add_fusion
  9.4 0.1 broadcast_in_dim.34
  9.5 0.9 fusion
  10.4 0.7 reshape.32
  11.0 6.4 %all-to-all-start = ((f32[8,2,896]{2,1,0:T(2,128)}), f32[8,2,896]{2,1,0:T(2,128)S(1)}, u32[]{:S(2)}, u32[]{:S(2)}) async-start(f32[8,2,896]{2,1,0:T(2,128)} %reshape.32), calls=%async_computation | async-start | bytes 114688 | tf_op jit(solution)/shard_map/all_to_all | solution.py:194
  17.4 0.0 all-reduce.2.cloned.1.call-start
  17.4 1.3 slice_select_fusion
  18.8 1.1 pad_maximum_fusion.lower_ref
  19.9 3.2 %all-to-all-done = f32[8,2,896]{2,1,0:T(2,128)S(1)} async-done(((f32[8,2,896]{2,1,0:T(2,128)}), f32[8,2,896]{2,1,0:T(2,128)S(1)}, u32[]{:S(2)}, u32[]{:S(2)}) %all-to-all-start) | async-done | bytes 57376 | tf_op jit(solution)/shard_map/all_to_all | solution.py:194
  23.1 7.6 %all_gather.3 = f32[32,2,896]{2,1,0:T(2,128)S(1)} all-gather(f32[8,2,896]{2,1,0:T(2,128)S(1)} %all-to-all-done), channel_id=1, replica_groups=mesh['tm'=8,'obs'=4] {'obs'}, dimensions={0}, use_global_device_ids=true | all-gather | bytes 286720 | tf_op jit(solution)/shard_map/all_gather | solution.py:195
  30.8 0.1 copy.25
  30.8 0.8 reshape.33.rows_ref
  31.7 0.1 copy.26
  31.8 0.1 broadcast_in_dim.36
  31.9 0.7 broadcast_in_dim.42.tag_ref
  32.6 0.6 broadcast_in_dim.38.label_ref
  33.2 31.4 %shard_map.128 = (f32[384,384]{1,0:T(8,128)}, f32[384,384]{1,0:T(8,128)}, f32[384,384]{1,0:T(8,128)}, f32[128,384]{1,0:T(8,128)}, f32[1,384]{1,0:T(1,128)}, /*in...) custom-call(f32[128,384]{1,0:T(8,128)} %reshape.33.rows_ref, ...), custom_call_target="tpu_custom_call" | custom-call | tf_op jit(solution)/shard_map/pallas_call | solution.py:201
  64.5 2.1 collective-permute-start
  66.6 1.9 collective-permute-start.1
  68.5 0.0 all-reduce.2.cloned.1.call-update
  68.6 1.9 collective-permute-start.2
  70.5 0.0 copy-start.8
  70.5 2.3 %pad_maximum_fusion.2 = f32[2,384,384]{2,1,0:T(8,128)} fusion(f32[1,384,384]{2,1,0:T(8,128)} %bitcast.17, f32[1,384,384]{2,1,0:T(8,128)} %bitcast.16), kind=kLoop, calls=%fused_computation.2 | loop fusion | flops 294912 | bytes 2359296 | tf_op jit(solution)/shard_map/stack | solution.py:214
  72.8 0.0 copy-done.8
  72.8 40.1 %psum.15.clift_ref = f32[1,128]{1,0:T(1,128)} all-reduce(f32[1,128]{1,0:T(1,128)S(1)} %copy-done.8), channel_id=1, replica_groups=mesh['tm'=8,'obs'=4] {'tm','obs'}, use_global_device_ids=true, to_apply=%region_2.3 | all-reduce | flops 128 | bytes 1024 | tf_op jit(solution)/shard_map/psum | solution.py:207
  112.9 75.2 %all-reduce.2.cloned.1.call-done.schur_ref = f32[128,128]{1,0:T(8,128)} async-done(((f32[128,128]{1,0:T(8,128)}), f32[128,128]{1,0:T(8,128)}) %all-reduce.2.cloned.1.call-update) | async-done | bytes 65552 | tf_op jit(solution)/shard_map/psum | solution.py:207
  188.1 9.4 %shard_map.130 = (f32[1,128]{1,0:T(1,128)}, f32[1,384]{1,0:T(1,128)}) custom-call(f32[128,128]{1,0:T(8,128)} %all-reduce.2.cloned.1.call-done.schur_ref, f32[1,128]{1,0:T(1,128)} %bitcast.21, f32[1,128]{1,0:T(1,128)} %bitcast.22, f32[1,128]{1,0:T(1,128)} %psum.15.clift_ref, f32[128,384]{1,0:T(8,128)} %get-tuple-element.23.side_ref, ...), custom_call_target="tpu_custom_call" | custom-call | tf_op jit(solution)/shard_map/pallas_call | solution.py:208
  197.6 0.0 collective-permute-done.2.lift_ref
  197.6 0.0 collective-permute-done.1.side_ref
  197.6 0.0 copy-start.4
  197.6 0.0 collective-permute-done.fill_ref
  197.6 0.0 copy-start.1
  197.6 0.5 copy-done.7
  198.1 0.1 copy-done.4
  198.2 0.2 copy-done.1
  198.4 3.8 %shard_map.129 = (f32[384,384]{1,0:T(8,128)}, f32[128,384]{1,0:T(8,128)}, f32[1,384]{1,0:T(1,128)}) custom-call(f32[384,384]{1,0:T(8,128)} %copy-done.1, f32[128,384]{1,0:T(8,128)} %copy-done.4, f32[1,384]{1,0:T(1,128)} %copy-done.7, f32[384,384]{1,0:T(8,128)} %get-tuple-element.25.blk_ref, f32[128,384]{1,0:T(8,128)} %get-tuple-element.26.tip_ref, ...), custom_call_target="tpu_custom_call" | custom-call | tf_op jit(solution)/shard_map/pallas_call | solution.py:211
  202.3 0.0 copy-done.2
  202.3 0.0 copy-start.5
  202.3 0.0 copy-start.6
  202.3 2.2 %pad_maximum_fusion.1 = f32[2,384,384]{2,1,0:T(8,128)} fusion(f32[1,384,384]{2,1,0:T(8,128)} %bitcast.18, f32[1,384,384]{2,1,0:T(8,128)S(1)} %bitcast.15), kind=kLoop, calls=%fused_computation.1 | loop fusion | flops 294912 | bytes 2359296 | tf_op jit(solution)/shard_map/stack | solution.py:213
  204.5 0.0 copy-done
  204.5 0.0 copy-done.3
  204.5 0.8 pad_maximum_fusion.3
  205.3 0.0 copy-done.5
  205.3 0.0 copy-done.6
  205.3 0.6 pad_maximum_fusion.4
  (6 shorter events, 0.0 us)
Async XLA Ops:
  11.0 12.1 %all-to-all-start = ((f32[8,2,896]{2,1,0:T(2,128)}), f32[8,2,896]{2,1,0:T(2,128)S(1)}, u32[]{:S(2)}, u32[]{:S(2)}) async-start(f32[8,2,896]{2,1,0:T(2,128)} %reshape.32), calls=%async_computation | async-start | bytes 114688 | tf_op jit(solution)/shard_map/all_to_all | solution.py:194
  17.4 170.7 %all-reduce.2.cloned.1.call-start = ((), (), s32[]{:S(2)}) async-start(), calls=%async_computation.1 | async-start | bytes 131072 | tf_op jit(solution)/shard_map/psum | solution.py:207
  64.5 133.0 %collective-permute-start = (f32[384,384]{1,0:T(8,128)}, f32[384,384]{1,0:T(8,128)S(1)}, u32[]{:S(2)}, u32[]{:S(2)}) collective-permute-start(f32[384,384]{1,0:T(8,128)} %get-tuple-element.22), channel_id=1, source_target_pairs={{1,0},{2,1},{3,2},{4,3},{5,4},{6,5},{7,6},{8,7},{9,8},{10,9},{11,1... | collective-permute-start | bytes 1769480 | tf_op jit(solution)/shard_map/ppermute | solution.py:172
  66.6 130.9 %collective-permute-start.1 = (f32[128,384]{1,0:T(8,128)}, f32[128,384]{1,0:T(8,128)S(1)}, u32[]{:S(2)}, u32[]{:S(2)}) collective-permute-start(f32[128,384]{1,0:T(8,128)} %get-tuple-element.23.side_ref), channel_id=1, source_target_pairs={{1,0},{2,1},{3,2},{4,3},{5,4},{6,5},{7,6},{8,7},{9,8},{10,9},{11,1... | collective-permute-start | bytes 589832 | tf_op jit(solution)/shard_map/ppermute | solution.py:172
  68.6 129.0 %collective-permute-start.2 = (f32[1,384]{1,0:T(1,128)}, f32[1,384]{1,0:T(1,128)S(1)}, u32[]{:S(2)}, u32[]{:S(2)}) collective-permute-start(f32[1,384]{1,0:T(1,128)} %get-tuple-element.24.lift_ref), channel_id=1, source_target_pairs={{1,0},{2,1},{3,2},{4,3},{5,4},{6,5},{7,6},{8,7},{9,8},{10,9},{11,1... | collective-permute-start | bytes 4616 | tf_op jit(solution)/shard_map/ppermute | solution.py:172
  70.5 2.4 %copy-start.8 = (f32[1,128]{1,0:T(1,128)S(1)}, f32[1,128]{1,0:T(1,128)}, u32[]{:S(2)}) copy-start(f32[1,128]{1,0:T(1,128)} %get-tuple-element.32) | copy-start | bytes 1540
  188.1 14.2 %copy-start.2 = (f32[384,384]{1,0:T(8,128)S(1)}, f32[384,384]{1,0:T(8,128)}, u32[]{:S(2)}) copy-start(f32[384,384]{1,0:T(8,128)} %get-tuple-element.21) | copy-start | bytes 1769476
  197.6 0.6 copy-start.7
  197.6 0.7 copy-start.4
  197.6 0.9 copy-start.1
  202.3 2.2 %copy-start = (f32[128,384]{1,0:T(8,128)S(1)}, f32[128,384]{1,0:T(8,128)}, u32[]{:S(2)}) copy-start(f32[128,384]{1,0:T(8,128)} %get-tuple-element.23.side_ref) | copy-start | bytes 589828
  202.3 2.2 %copy-start.3 = (f32[128,384]{1,0:T(8,128)S(1)}, f32[128,384]{1,0:T(8,128)}, u32[]{:S(2)}) copy-start(f32[128,384]{1,0:T(8,128)} %get-tuple-element.30) | copy-start | bytes 589828
  202.3 3.0 %copy-start.5 = (f32[1,384]{1,0:T(1,128)S(1)}, f32[1,384]{1,0:T(1,128)}, u32[]{:S(2)}) copy-start(f32[1,384]{1,0:T(1,128)} %get-tuple-element.34) | copy-start | bytes 4612
  202.3 3.0 %copy-start.6 = (f32[1,384]{1,0:T(1,128)S(1)}, f32[1,384]{1,0:T(1,128)}, u32[]{:S(2)}) copy-start(f32[1,384]{1,0:T(1,128)} %get-tuple-element.35) | copy-start | bytes 4612
Sparse Core Ops, SparseCore 0:
  68.7 119.3 all-reduce.1

commit v2 on v1

--- a/solution.py
+++ b/solution.py
@@ -83,21 +83,17 @@
 
 def local_kernel(
     rows_ref, tag_ref, label_ref, prior_ref, lower_ref, tip_ref, rhs_ref,
-    factor_ref, fill_ref, newlow_ref, side_ref, lift_ref, partblk_ref, parttip_ref, partrhs_ref,
-    inv_ref, terms_ref, tlift_ref,
-    gram, work, y,
+    factor_ref, low_ref, y_ref, inv_ref, terms_ref, pack_ref,
+    gram, work, flat,
 ):
     B = prior_ref.shape[1]
     K = tip_ref.shape[1]
     nb = B // T
-    tags = tag_ref[...]
     even = label_ref[0:1, 0:1]
-    rows = rows_ref[...]
-    identity = eye(B)
-    chosen = jnp.where(tags == even, rows, 0.0)
-    gram[...] = dot_tn(chosen, chosen) + prior_ref[0:1, :] * identity
+    chosen = jnp.where(tag_ref[...] == even, rows_ref[...], 0.0)
+    gram[...] = dot_tn(chosen, chosen) + prior_ref[0:1, :] * eye(B)
     inv_ref[...] = jnp.zeros((B, B), jnp.float32)
-    factor_ref[...] = jnp.zeros((B, B), jnp.float32)
+    factor_ref[0] = jnp.zeros((B, B), jnp.float32)
     upper = upper_mask(T)
     for b in range(nb):
         lo, hi = b * T, (b + 1) * T
@@ -105,64 +101,140 @@
         work[:, T:] = eye(T)
         factor_tile(work)
         inv = jnp.where(upper.T, work[:, T:], 0.0)
-        factor_ref[lo:hi, lo:hi] = jnp.where(upper, work[:, :T], 0.0).T
+        factor_ref[0, lo:hi, lo:hi] = jnp.where(upper, work[:, :T], 0.0).T
         inv_ref[lo:hi, lo:hi] = inv
         if b > 0:
-            inv_ref[lo:hi, :lo] = -dot_nn(inv, dot_nn(factor_ref[lo:hi, :lo], inv_ref[:lo, :lo]))
+            inv_ref[lo:hi, :lo] = -dot_nn(inv, dot_nn(factor_ref[0, lo:hi, :lo], inv_ref[:lo, :lo]))
         if b + 1 < nb:
             upper_rest = dot_nn(inv, gram[lo:hi, hi:])
             gram[hi:, hi:] = gram[hi:, hi:] - dot_tn(upper_rest, upper_rest)
-            factor_ref[hi:, lo:hi] = upper_rest.T
+            factor_ref[0, hi:, lo:hi] = upper_rest.T
     linv = inv_ref[...]
-    y[:B, :] = lower_ref[1]
-    y[B : B + K, :] = tip_ref[0]
-    y[B + K :, :] = jnp.concatenate([rhs_ref[0:1, :], jnp.zeros((7, B), jnp.float32)], axis=0)
-    y[...] = dot_nt(y[...], linv)
-    fill = dot_nn(linv, lower_ref[0])
-    fill_ref[...] = fill
-    side = y[B : B + K, :]
-    side_ref[...] = side
-    lift_ref[...] = y[B + K : B + K + 1, :]
-    xt = y[:B, :]
-    terms_ref[...] = (
+    low = jnp.where(label_ref[1:2, 0:1] == 0.0, 0.0, lower_ref[0])
+    fill = dot_nn(linv, low)
+    low_ref[0] = fill
+    pack_ref[:B, :] = fill
+    y_ref[:B, :] = lower_ref[1]
+    y_ref[B : B + K, :] = tip_ref[0]
+    y_ref[B + K :, :] = jnp.concatenate([rhs_ref[0:1, :], jnp.zeros((7, B), jnp.float32)], axis=0)
+    y_ref[...] = dot_nt(y_ref[...], linv)
+    side = y_ref[B : B + K, :]
+    pack_ref[B:, :] = y_ref[B:, :]
+    flat[:K, :] = (
         dot_nt(tip_ref[0], tip_ref[0]) + dot_nt(tip_ref[1], tip_ref[1]) - dot_nt(side, side)
     )
-    tlift_ref[...] = dot_nt(y[B + K :, :], side)[0:1, :]
-    newlow_ref[...] = -dot_nn(xt, fill)
-    back = dot_nt(y[...], xt)
-    chosen_odd = jnp.where(tags == even + 1.0, rows, 0.0)
-    partblk_ref[...] = dot_tn(chosen_odd, chosen_odd) + prior_ref[1:2, :] * identity - back[:B]
-    parttip_ref[...] = tip_ref[1] - back[B : B + K]
-    partrhs_ref[...] = rhs_ref[1:2, :] - back[B + K : B + K + 1]
-
-
-def finish_kernel(fill_ref, side_ref, lift_ref, blk_ref, tip_ref, rhs_ref, oblk, otip, orhs):
-    fill = fill_ref[...]
-    oblk[...] = blk_ref[...] - dot_tn(fill, fill)
-    otip[...] = tip_ref[...] - dot_nn(side_ref[...], fill)
-    lift = jnp.concatenate([lift_ref[...]] * 8, axis=0)
-    orhs[...] = rhs_ref[...] - dot_nn(lift, fill)[0:1, :]
-
-
-def tip_kernel(schur_ref, prior_ref, crhs_ref, clift_ref, side_ref, lift_ref, inv_ref, sol_ref, est_ref, work):
-    work[:, :T] = schur_ref[...] + prior_ref[...] * eye(T)
+    flat[K : K + 8, :] = dot_nt(y_ref[B + K :, :], side)
+    flat[K + 8 :, :] = jnp.zeros((flat.shape[0] - K - 8, K), jnp.float32)
+    chunk = terms_ref.shape[1]
+    for i in range(terms_ref.shape[0]):
+        terms_ref[i] = flat[i * chunk : (i + 1) * chunk, :] if i * chunk <= K else jnp.zeros((chunk, K), jnp.float32)
+
+
+def reduce_kernel(x_ref, out_ref, stage, own, full, send_a, recv_a, send_b, recv_b):
+    n_tm, n_obs = lax.axis_size("tm"), lax.axis_size("obs")
+    n = n_tm * n_obs
+    me = lax.axis_index("tm") * n_obs + lax.axis_index("obs")
+
+    def place(k):
+        peer = lax.rem(me + k, n)
+        return peer, (peer // n_obs, lax.rem(peer, n_obs))
+
+    def scatter(k):
+        peer, where = place(k)
+        return pltpu.make_async_remote_copy(
+            src_ref=x_ref.at[peer], dst_ref=stage.at[k], send_sem=send_a.at[k], recv_sem=recv_a.at[k],
+            device_id=where, device_id_type=pl.DeviceIdType.MESH,
+        )
+
+    def gather(k):
+        _, where = place(k)
+        return pltpu.make_async_remote_copy(
+            src_ref=own, dst_ref=full.at[k], send_sem=send_b.at[k], recv_sem=recv_b.at[k],
+            device_id=where, device_id_type=pl.DeviceIdType.MESH,
+        )
+
+    barrier = pltpu.get_barrier_semaphore()
+
+    @pl.loop(1, n)
+    def _(k):
+        _, where = place(k)
+        pl.semaphore_signal(barrier, inc=1, device_id=where, device_id_type=pl.DeviceIdType.MESH)
+
+    pl.semaphore_wait(barrier, n - 1)
+
+    @pl.loop(1, n)
+    def _(k):
+        scatter(k).start()
+
+    own[...] = x_ref[me]
+
+    @pl.loop(1, n)
+    def _(k):
+        scatter(k).wait()
+        own[...] = own[...] + stage[k]
+
+    @pl.loop(1, n)
+    def _(k):
+        gather(k).start()
+
+    out_ref[me] = own[...]
+
+    @pl.loop(1, n)
+    def _(k):
+        gather(k).wait()
+        out_ref[lax.rem(me - k + n, n)] = full[k]
+
+
+def final_kernel(
+    rows_ref, tag_ref, label_ref, prior_ref, tip_ref, rhs_ref, y_ref, inv_ref, sum_ref,
+    tprior_ref, crhs_ref, next_ref, low_in, blk_in, fill_ref,
+    blk_ref, low_ref, otip_ref, res_ref, sol_ref,
+    work, flat,
+):
+    B = prior_ref.shape[1]
+    K = tip_ref.shape[1]
+    chunk = sum_ref.shape[1]
+    for i in range(sum_ref.shape[0]):
+        if i * chunk <= K:
+            flat[i * chunk : (i + 1) * chunk, :] = sum_ref[i]
+    work[:, :T] = flat[:K, :] + tprior_ref[...] * eye(T)
     work[:, T:] = eye(T)
+    xt = y_ref[:B, :]
+    back = dot_nt(y_ref[...], xt)
+    chosen = jnp.where(tag_ref[...] == label_ref[0:1, 0:1] + 1.0, rows_ref[...], 0.0)
+    nfill = next_ref[:B, :]
+    blk_ref[0] = (
+        dot_tn(chosen, chosen) + prior_ref[1:2, :] * eye(B) - back[:B] - dot_tn(nfill, nfill)
+    )
+    right = dot_nn(next_ref[B:, :], nfill)
+    side = y_ref[B : B + K, :]
+    otip_ref[0] = side
+    otip_ref[1] = tip_ref[1] - back[B : B + K] - right[:K]
+    res_ref[1:2, :] = rhs_ref[1:2, :] - back[B + K : B + K + 1] - right[K : K + 1]
+    low_ref[0] = -dot_nn(xt, fill_ref[...])
     factor_tile(work)
     inv = jnp.where(upper_mask(T).T, work[:, T:], 0.0)
-    vec = jnp.concatenate([crhs_ref[...] - clift_ref[...]] * 8, axis=0)
+    vec = jnp.concatenate([crhs_ref[...] - flat[K : K + 1, :]] * 8, axis=0)
     sol = dot_nn(dot_nt(vec, inv), inv)
     sol_ref[...] = sol[0:1, :]
-    lift = jnp.concatenate([lift_ref[...]] * 8, axis=0)
-    pulled = lift - dot_nn(sol, side_ref[...])
-    est_ref[...] = dot_nn(pulled, inv_ref[...])[0:1, :]
-
-
-def call(kernel, outs, scratch=()):
+    lift = jnp.concatenate([y_ref[B + K : B + K + 1, :]] * 8, axis=0)
+    res_ref[0:1, :] = dot_nn(lift - dot_nn(sol, side), inv_ref[...])[0:1, :]
+
+
+def call(kernel, outs, scratch=(), in_specs=None, out_specs=None, aliases={}, sems=(), cost=None, grid=None, **params):
+    extra = {} if grid is None else {"grid": grid}
+    if in_specs is not None:
+        extra["in_specs"] = in_specs
+    if out_specs is not None:
+        extra["out_specs"] = out_specs
     return pl.pallas_call(
         kernel,
         out_shape=[jax.ShapeDtypeStruct(s, jnp.float32) for s in outs],
-        scratch_shapes=[pltpu.VMEM(s, jnp.float32) for s in scratch],
-        compiler_params=pltpu.CompilerParams(vmem_limit_bytes=56 << 20),
+        scratch_shapes=[pltpu.VMEM(s, jnp.float32) for s in scratch]
+        + [pltpu.SemaphoreType.DMA((s,)) for s in sems],
+        input_output_aliases=aliases,
+        compiler_params=pltpu.CompilerParams(vmem_limit_bytes=56 << 20, **params),
+        **extra,
     )
 
 
@@ -195,27 +267,55 @@
     gathered = lax.all_gather(arrived, "obs", axis=0, tiled=True)
     rows_part = gathered[:, :, : R * B].reshape(-1, B)
     tags = jnp.broadcast_to(gathered[:, :, R * B :][:, :, None, :1], gathered.shape[:2] + (R, 1)).reshape(-1, 1)
-    label = jnp.full((8, 128), 2 * member_index + 1, jnp.float32)
-    masked_lower = jnp.where(position == 0, jnp.zeros_like(lower_coupling[0]), lower_coupling[0])
-    lower = jnp.stack([masked_lower, lower_coupling[1]])
-    (factor, fill, newlow, side, lift, pblk, ptip, prhs, inv, terms, tlift) = call(
+    label = jnp.concatenate(
+        [
+            jnp.full((1, 128), 2 * member_index + 1, jnp.float32),
+            jnp.full((7, 128), position, jnp.float32),
+        ]
+    )
+    n = groups * lax.axis_size("obs")
+    chunk = -(-(K + 1) // n)
+    used = -(-(n * chunk + 8) // 8) * 8
+    flat_rows = max(used, K + 16)
+    first = pl.BlockSpec((1, B, B), lambda i: (0, 0, 0))
+    second = pl.BlockSpec((1, B, B), lambda i: (1, 0, 0))
+
+    def whole(shape):
+        return pl.BlockSpec(shape, lambda i: (0,) * len(shape))
+
+    rows_args = (rows_part, tags, label, prior_diag)
+    wide = (B + K + 8, B)
+    block, low, y, inv, terms, pack = call(
         local_kernel,
-        [(B, B), (B, B), (B, B), (K, B), (1, B), (B, B), (K, B), (1, B), (B, B), (K, K), (1, K)],
-        [(B, B), (T, 2 * T), (B + K + 8, B)],
-    )(rows_part, tags, label, prior_diag, lower, tip_coupling, time_rhs)
-    nfill, nside, nlift = shifted((fill, side, lift), ("tm", "obs"), -1)
-    schur, slift = lax.psum((terms, tlift), ("tm", "obs"))
-    sol, est = call(tip_kernel, [(1, K), (1, B)], [(T, 2 * T)])(
-        schur, tip_prior[None, :], tip_rhs[None, :], slift, side, lift, inv
-    )
-    nblk, ntip, nrhs = call(finish_kernel, [(B, B), (K, B), (1, B)])(nfill, nside, nlift, pblk, ptip, prhs)
-    return (
-        jnp.stack([factor, nblk]),
-        jnp.stack([fill, newlow]),
-        jnp.stack([side, ntip]),
-        jnp.concatenate([est, nrhs], axis=0),
-        sol[0],
-    )
+        [(2, B, B), (2, B, B), wide, (B, B), (n, chunk, K), wide],
+        [(B, B), (T, 2 * T), (flat_rows, K)],
+        grid=(1,),
+        in_specs=[whole(v.shape) for v in (*rows_args, lower_coupling, tip_coupling, time_rhs)],
+        out_specs=[first, first, whole(wide), whole((B, B)), whole((n, chunk, K)), whole(wide)],
+    )(*rows_args, lower_coupling, tip_coupling, time_rhs)
+    following = shifted(pack, ("tm", "obs"), -1)
+    total = call(
+        reduce_kernel,
+        [(n, chunk, K)],
+        [(n, chunk, K), (chunk, K), (n, chunk, K)],
+        sems=[n, n, n, n],
+        in_specs=[VMEM],
+        out_specs=[VMEM],
+        collective_id=1,
+        has_side_effects=True,
+    )(terms)[0]
+    any_spec = pl.BlockSpec(memory_space=pl.ANY)
+    plain = (*rows_args, tip_coupling, time_rhs, y, inv, total, tip_prior[None, :], tip_rhs[None, :], following)
+    block, low, tip, result, sol = call(
+        final_kernel,
+        [(2, B, B), (2, B, B), (2, K, B), (2, B), (1, K)],
+        [(T, 2 * T), (flat_rows, K)],
+        grid=(1,),
+        in_specs=[whole(v.shape) for v in plain] + [any_spec, any_spec, whole((B, B))],
+        out_specs=[second, second, whole((2, K, B)), whole((2, B)), whole((1, K))],
+        aliases={len(plain): 1, len(plain) + 1: 0},
+    )(*plain, low, block, pack[:B])
+    return block, low, tip, result, sol[0]
 
 
 def solution(mesh):

time: 213 us -> 93.5 us (0.44)
  waiting for transfers between devices: 78.5 us -> 5.7 us
  blocking collectives: 47.7 us -> 7.61 us
  Pallas kernels: 44.6 us -> 61.1 us
  between operations: 14.2 us -> 0.7 us
  other arithmetic: 10.5 us -> 2.23 us
  starting transfers between devices: 12.3 us -> 8.43 us
    psum x1 -> x0, waiting for transfers between devices: 75.2 us -> none  [local(): schur, slift = lax.psum((terms, tlift), ('tm', 'obs'))]
    psum x1 -> x0, blocking collectives: 40.1 us -> none  [local(): schur, slift = lax.psum((terms, tlift), ('tm', 'obs'))]
    pallas_call x3, Pallas kernels: 44.6 us -> 61.1 us  [the longest x1 27.8 us: local(): call(local_kernel, [(2, B, B), (2, B, B), wide, (B, B), (n, chunk, K), wi...]
    another operation x4 -> x0, other arithmetic: 6.4 us -> none  [the longest x1 2.34 us: local(): jnp.stack([fill, newlow])]
    ppermute x3 -> x1, starting transfers between devices: 5.9 us -> 2.06 us  [shifted(): lax.ppermute(value, axis, [(source, source + steps) for source in range(f...]
    all_to_all x1, waiting for transfers between devices: 3.23 us -> 5.69 us  [local(): lax.all_to_all(outgoing, 'tm', split_axis=0, concat_axis=0, tiled=True)]
  transfers between devices with their start and end apart: 5 -> 2, of which waited for: 2 -> 1; matrix products, arithmetic and copies ran while one was open for 2% -> 2% of each run, Pallas kernels for 4% -> 20%
where the time goes in v2:
time: 93.5 us; the launch traced here: 92.7 us
  Pallas kernels  61.1 us (65%)
  starting transfers between devices  8.43 us (9%)
  blocking collectives  7.61 us (8%)
  local copies, waits for them, and re-layouts  6.06 us (6%)
  waiting for transfers between devices  5.7 us (6%)
  other arithmetic  2.23 us (2%)
    pallas_call x1, Pallas kernels, local(): call(local_kernel, [(2, B, B), (2, B, B), wide, (B, B), (n, chunk, K), wi...  27.8 us
    pallas_call x1, Pallas kernels, local(): call(reduce_kernel, [(n, chunk, K)], [(n, chunk, K), (chunk, K), (n, chun...  18.7 us
    pallas_call x1, Pallas kernels, local(): call(final_kernel, [(2, B, B), (2, B, B), (2, K, B), (2, B), (1, K)], [(T...  14.6 us
    all_gather x1, blocking collectives, local(): gathered = lax.all_gather(arrived, 'obs', axis=0, tiled=True)  7.61 us
    all_to_all x1, starting transfers between devices, local(): lax.all_to_all(outgoing, 'tm', split_axis=0, concat_axis=0, tiled=True)  6.37 us
    all_to_all x1, waiting for transfers between devices, local(): lax.all_to_all(outgoing, 'tm', split_axis=0, concat_axis=0, tiled=True)  5.69 us
    ppermute x1, starting transfers between devices, shifted(): lax.ppermute(value, axis, [(source, source + steps) for source in range(f...  2.06 us
    slice x1, local copies, waits for them, and re-layouts, local(): pack[:B]  1.92 us
  transfers between devices with their start and end apart: 2, of which 1 were waited for; matrix products, arithmetic and copies ran while one was open for 2% of the time, Pallas kernels for 20%

profile of v2, /device:TPU:1, one launch (start us, length us, event | category | flops | bytes accessed | tf_op | source)
XLA Modules:
  0.0 92.7 jit_solution(4560681226258416580)
XLA Ops:
  0.6 0.7 add_bitcast_fusion
  1.3 0.9 convert_reduce_fusion
  2.2 0.7 multiply_add_fusion
  2.9 0.1 broadcast_in_dim.32
  2.9 0.9 fusion
  3.8 0.7 reshape.33
  4.5 6.4 %all-to-all-start = ((f32[8,2,896]{2,1,0:T(2,128)}), f32[8,2,896]{2,1,0:T(2,128)S(1)}, u32[]{:S(2)}, u32[]{:S(2)}) async-start(f32[8,2,896]{2,1,0:T(2,128)} %reshape.33), calls=%async_computation | async-start | bytes 114688 | tf_op jit(solution)/shard_map/all_to_all | solution.py:266
  10.9 5.7 %all-to-all-done = f32[8,2,896]{2,1,0:T(2,128)S(1)} async-done(((f32[8,2,896]{2,1,0:T(2,128)}), f32[8,2,896]{2,1,0:T(2,128)S(1)}, u32[]{:S(2)}, u32[]{:S(2)}) %all-to-all-start) | async-done | bytes 57376 | tf_op jit(solution)/shard_map/all_to_all | solution.py:266
  16.6 7.6 %all_gather.3 = f32[32,2,896]{2,1,0:T(2,128)S(1)} all-gather(f32[8,2,896]{2,1,0:T(2,128)S(1)} %all-to-all-done), channel_id=1, replica_groups=mesh['tm'=8,'obs'=4] {'obs'}, dimensions={0}, use_global_device_ids=true | all-gather | bytes 286720 | tf_op jit(solution)/shard_map/all_gather | solution.py:267
  24.2 0.1 copy.30
  24.3 0.8 reshape.34.rows_ref
  25.1 0.1 copy.31
  25.2 0.1 broadcast_in_dim.34
  25.3 0.7 broadcast_in_dim.39.tag_ref
  26.1 0.7 concatenate.10.label_ref
  26.7 27.8 %shard_map.128 = (f32[2,384,384]{2,1,0:T(8,128)}, f32[2,384,384]{2,1,0:T(8,128)}, f32[520,384]{1,0:T(8,128)}, f32[384,384]{1,0:T(8,128)}, f32[32,5,128]{2,1,0:T(8,128)}, /*index=5*/f32[520,384]{1,0:T(8,128)}) custom-call(f32[128,384]{1,0:T(8,128)} %reshape.34.rows_ref, f32[128,1]{1,0:T(8,128)} %broadcast_in_dim.39.tag_ref, f32[8,128]{1,0:T(8,128)} %concatenate.10.label_ref, ...), custom_call_target="tpu_custom_call" | custom-call | tf_op jit(solution)/shard_map/pallas_call | solution.py:288
  54.6 2.1 %collective-permute-start = (f32[520,384]{1,0:T(8,128)}, f32[520,384]{1,0:T(8,128)S(1)}, u32[]{:S(2)}, u32[]{:S(2)}) collective-permute-start(f32[520,384]{1,0:T(8,128)} %get-tuple-element.19), channel_id=1, source_target_pairs={{1,0},{2,1},{3,2},{4,3},{5,4},{6,5},{7,6},{8,7},{9,8},{10,9},{11,1... | collective-permute-start | bytes 2396168 | tf_op jit(solution)/shard_map/ppermute | solution.py:244
  56.6 1.9 %slice.13.fill_ref = f32[384,384]{1,0:T(8,128)} slice(f32[520,384]{1,0:T(8,128)} %get-tuple-element.19), slice={[0:384], [0:384]} | slice | bytes 1179648 | tf_op jit(solution)/shard_map/slice | solution.py:317
  58.5 18.7 %shard_map.129.sum_ref = f32[32,5,128]{2,1,0:T(8,128)} custom-call(f32[32,5,128]{2,1,0:T(8,128)} %get-tuple-element.18.x_ref), custom_call_target="tpu_custom_call" | custom-call | tf_op jit(solution)/shard_map/pallas_call | solution.py:297
  77.3 0.0 collective-permute-done.next_ref
  77.3 0.0 copy-start
  77.3 0.9 copy-done
  78.2 14.6 %shard_map.130 = (f32[2,384,384]{2,1,0:T(8,128)}, f32[2,384,384]{2,1,0:T(8,128)}, f32[2,128,384]{2,1,0:T(8,128)}, f32[2,384]{1,0:T(2,128)}, f32[1,128]{1,0:T(1,128)}) custom-call(f32[128,384]{1,0:T(8,128)} %reshape.34.rows_ref, f32[128,1]{1,0:T(8,128)} %broadcast_in_dim.39.tag_ref, ...), custom_call_target="tpu_custom_call", output_to_operand_aliasing={{1}: (12, {}), {0}: (13, {})} | custom-call | tf_op jit(solution)/shard_map/pallas_call | solution.py:309
  (3 shorter events, 0.0 us)
Async XLA Ops:
  4.5 12.1 %all-to-all-start = ((f32[8,2,896]{2,1,0:T(2,128)}), f32[8,2,896]{2,1,0:T(2,128)S(1)}, u32[]{:S(2)}, u32[]{:S(2)}) async-start(f32[8,2,896]{2,1,0:T(2,128)} %reshape.33), calls=%async_computation | async-start | bytes 114688 | tf_op jit(solution)/shard_map/all_to_all | solution.py:266
  54.6 22.7 %collective-permute-start = (f32[520,384]{1,0:T(8,128)}, f32[520,384]{1,0:T(8,128)S(1)}, u32[]{:S(2)}, u32[]{:S(2)}) collective-permute-start(f32[520,384]{1,0:T(8,128)} %get-tuple-element.19), channel_id=1, source_target_pairs={{1,0},{2,1},{3,2},{4,3},{5,4},{6,5},{7,6},{8,7},{9,8},{10,9},{11,1... | collective-permute-start | bytes 2396168 | tf_op jit(solution)/shard_map/ppermute | solution.py:244
  77.3 0.9 copy-start

commit v3 on v2

--- a/solution.py
+++ b/solution.py
@@ -57,7 +57,6 @@
         for i in range(PANEL):
             pivot = jnp.broadcast_to(cols[i][i : i + 1, :], (PANEL, T))
             root = lax.rsqrt(pivot)
-            root = root * (1.5 - 0.5 * pivot * root * root)
             scale = jnp.where(sub_t == i, root, scale)
             if i + 1 < PANEL:
                 mult = jnp.where(sub_t > i, cols[i] * (root * root), 0.0)
@@ -90,7 +89,7 @@
     K = tip_ref.shape[1]
     nb = B // T
     even = label_ref[0:1, 0:1]
-    chosen = jnp.where(tag_ref[...] == even, rows_ref[...], 0.0)
+    chosen = jnp.where(tag_ref[:, :1] == even, rows_ref[...], 0.0)
     gram[...] = dot_tn(chosen, chosen) + prior_ref[0:1, :] * eye(B)
     inv_ref[...] = jnp.zeros((B, B), jnp.float32)
     factor_ref[0] = jnp.zeros((B, B), jnp.float32)
@@ -185,10 +184,10 @@
         out_ref[lax.rem(me - k + n, n)] = full[k]
 
 
-def final_kernel(
+def tip_kernel(
     rows_ref, tag_ref, label_ref, prior_ref, tip_ref, rhs_ref, y_ref, inv_ref, sum_ref,
-    tprior_ref, crhs_ref, next_ref, low_in, blk_in, fill_ref,
-    blk_ref, low_ref, otip_ref, res_ref, sol_ref,
+    tprior_ref, crhs_ref, fill_ref, low_in,
+    low_ref, blk_ref, otip_ref, res_ref, sol_ref,
     work, flat,
 ):
     B = prior_ref.shape[1]
@@ -201,16 +200,12 @@
     work[:, T:] = eye(T)
     xt = y_ref[:B, :]
     back = dot_nt(y_ref[...], xt)
-    chosen = jnp.where(tag_ref[...] == label_ref[0:1, 0:1] + 1.0, rows_ref[...], 0.0)
-    nfill = next_ref[:B, :]
-    blk_ref[0] = (
-        dot_tn(chosen, chosen) + prior_ref[1:2, :] * eye(B) - back[:B] - dot_tn(nfill, nfill)
-    )
-    right = dot_nn(next_ref[B:, :], nfill)
+    chosen = jnp.where(tag_ref[:, :1] == label_ref[0:1, 0:1] + 1.0, rows_ref[...], 0.0)
+    blk_ref[...] = dot_tn(chosen, chosen) + prior_ref[1:2, :] * eye(B) - back[:B]
     side = y_ref[B : B + K, :]
     otip_ref[0] = side
-    otip_ref[1] = tip_ref[1] - back[B : B + K] - right[:K]
-    res_ref[1:2, :] = rhs_ref[1:2, :] - back[B + K : B + K + 1] - right[K : K + 1]
+    otip_ref[1] = tip_ref[1] - back[B : B + K]
+    res_ref[1:2, :] = rhs_ref[1:2, :] - back[B + K : B + K + 1]
     low_ref[0] = -dot_nn(xt, fill_ref[...])
     factor_tile(work)
     inv = jnp.where(upper_mask(T).T, work[:, T:], 0.0)
@@ -219,6 +214,94 @@
     sol_ref[...] = sol[0:1, :]
     lift = jnp.concatenate([y_ref[B + K : B + K + 1, :]] * 8, axis=0)
     res_ref[0:1, :] = dot_nn(lift - dot_nn(sol, side), inv_ref[...])[0:1, :]
+
+
+def finish_kernel(next_ref, part_ref, tip_in, res_in, blk_in, blk_ref, otip_ref, res_ref):
+    B = part_ref.shape[1]
+    K = tip_in.shape[1]
+    nfill = next_ref[:B, :]
+    blk_ref[0] = part_ref[...] - dot_tn(nfill, nfill)
+    right = dot_nn(next_ref[B:, :], nfill)
+    otip_ref[0] = tip_in[0] - right[:K]
+    res_ref[0:1, :] = res_in[0:1, :]
+    res_ref[1:2, :] = res_in[1:2, :] - right[K : K + 1]
+
+
+def pack_kernel(rows_ref, owner_ref, member_ref, out_ref):
+    groups = out_ref.shape[0]
+    blocks, width = rows_ref.shape
+    owners = owner_ref[...]
+    named = (lax.broadcasted_iota(jnp.int32, (blocks, groups), 1) == owners).astype(jnp.float32)
+    before = lax.broadcasted_iota(jnp.int32, (blocks, blocks), 1) < lax.broadcasted_iota(
+        jnp.int32, (blocks, blocks), 0
+    )
+    rank = jnp.sum(dot_nn(before.astype(jnp.float32), named) * named, axis=1, keepdims=True)
+    slot = owners.astype(jnp.float32) * CAP + rank
+    spots = lax.broadcasted_iota(jnp.int32, (blocks, groups * CAP), 1).astype(jnp.float32)
+    pick = (spots == slot).astype(jnp.float32)
+    tag = jnp.broadcast_to(member_ref[...].astype(jnp.float32) + 1.0, (blocks, 128))
+    rows = dot_tn(pick, rows_ref[...])
+    tags = dot_tn(pick, tag)
+    for g in range(groups):
+        out_ref[g, :, :width] = rows[g * CAP : (g + 1) * CAP, :]
+        out_ref[g, :, width:] = tags[g * CAP : (g + 1) * CAP, :]
+
+
+def route_kernel(x_ref, rows_ref, tags_ref, stage, landed, local_sem, send_a, recv_a, send_b, recv_b):
+    groups, n_obs = lax.axis_size("tm"), lax.axis_size("obs")
+    t, o = lax.axis_index("tm"), lax.axis_index("obs")
+    mesh_id = pl.DeviceIdType.MESH
+
+    def toward(k):
+        peer = lax.rem(t + k, groups)
+        return pltpu.make_async_remote_copy(
+            src_ref=x_ref.at[peer], dst_ref=stage.at[k], send_sem=send_a.at[k], recv_sem=recv_a.at[k],
+            device_id=(peer, o), device_id_type=mesh_id,
+        )
+
+    def across(k):
+        return pltpu.make_async_remote_copy(
+            src_ref=stage, dst_ref=landed.at[k], send_sem=send_b.at[k], recv_sem=recv_b.at[k],
+            device_id=(t, lax.rem(o + k, n_obs)), device_id_type=mesh_id,
+        )
+
+    barrier = pltpu.get_barrier_semaphore()
+
+    @pl.loop(1, groups)
+    def _(k):
+        pl.semaphore_signal(barrier, inc=1, device_id=(lax.rem(t + k, groups), o), device_id_type=mesh_id)
+
+    @pl.loop(1, n_obs)
+    def _(k):
+        pl.semaphore_signal(barrier, inc=1, device_id=(t, lax.rem(o + k, n_obs)), device_id_type=mesh_id)
+
+    own = pltpu.make_async_copy(x_ref.at[t], stage.at[0], local_sem.at[0])
+    own.start()
+    pl.semaphore_wait(barrier, groups + n_obs - 2)
+
+    @pl.loop(1, groups)
+    def _(k):
+        toward(k).start()
+
+    own.wait()
+
+    @pl.loop(1, groups)
+    def _(k):
+        toward(k).wait()
+
+    for k in range(1, n_obs):
+        across(k).start()
+    B = rows_ref.shape[1]
+    half = n_obs * groups * CAP
+    for k in range(n_obs):
+        if k:
+            across(k).wait()
+        for g in range(groups):
+            at = (k * groups + g) * CAP
+            piece = landed[k, g] if k else stage[g]
+            for r in range(R):
+                rows_ref[r * half + at : r * half + at + CAP, :] = piece[:, r * B : (r + 1) * B]
+                tags_ref[r * half + at : r * half + at + CAP, :] = piece[:, R * B :]
 
 
 def call(kernel, outs, scratch=(), in_specs=None, out_specs=None, aliases={}, sems=(), cost=None, grid=None, **params):
@@ -233,6 +316,7 @@
         scratch_shapes=[pltpu.VMEM(s, jnp.float32) for s in scratch]
         + [pltpu.SemaphoreType.DMA((s,)) for s in sems],
         input_output_aliases=aliases,
+        cost_estimate=cost,
         compiler_params=pltpu.CompilerParams(vmem_limit_bytes=56 << 20, **params),
         **extra,
     )
@@ -252,21 +336,20 @@
     member_index = lax.axis_index("obs")
     B = prior_diag.shape[1]
     K = tip_coupling.shape[1]
-    blocks = obs_rows.shape[0]
-    owners = obs_owner[:, 0]
-    ordinal = jnp.arange(blocks, dtype=jnp.int32)
-    earlier = (owners[:, None] == owners[None, :]) & (ordinal[None, :] < ordinal[:, None])
-    slot_rank = jnp.sum(earlier.astype(jnp.int32), axis=1)
-    slot_index = owners * CAP + slot_rank
-    pick = (jnp.arange(groups * CAP, dtype=jnp.int32)[:, None] == slot_index[None, :]).astype(jnp.float32)
-    tagged = jnp.concatenate(
-        [obs_rows, jnp.broadcast_to(obs_member.astype(jnp.float32) + 1.0, (blocks, 128))], axis=1
-    )
-    outgoing = jnp.dot(pick, tagged, precision=HI).reshape(groups, CAP, -1)
-    arrived = lax.all_to_all(outgoing, "tm", split_axis=0, concat_axis=0, tiled=True)
-    gathered = lax.all_gather(arrived, "obs", axis=0, tiled=True)
-    rows_part = gathered[:, :, : R * B].reshape(-1, B)
-    tags = jnp.broadcast_to(gathered[:, :, R * B :][:, :, None, :1], gathered.shape[:2] + (R, 1)).reshape(-1, 1)
+    members = lax.axis_size("obs")
+    width = R * B + 128
+    outgoing = call(pack_kernel, [(groups, CAP, width)])(obs_rows, obs_owner, obs_member)[0]
+    count = members * groups * CAP * R
+    rows_part, tags = call(
+        route_kernel,
+        [(count, B), (count, 128)],
+        [(groups, CAP, width), (members, groups, CAP, width)],
+        sems=[1, groups, groups, members, members],
+        in_specs=[VMEM],
+        out_specs=[VMEM, VMEM],
+        collective_id=2,
+        has_side_effects=True,
+    )(outgoing)
     label = jnp.concatenate(
         [
             jnp.full((1, 128), 2 * member_index + 1, jnp.float32),
@@ -293,7 +376,6 @@
         in_specs=[whole(v.shape) for v in (*rows_args, lower_coupling, tip_coupling, time_rhs)],
         out_specs=[first, first, whole(wide), whole((B, B)), whole((n, chunk, K)), whole(wide)],
     )(*rows_args, lower_coupling, tip_coupling, time_rhs)
-    following = shifted(pack, ("tm", "obs"), -1)
     total = call(
         reduce_kernel,
         [(n, chunk, K)],
@@ -304,17 +386,28 @@
         collective_id=1,
         has_side_effects=True,
     )(terms)[0]
+    pack_late, total_late = lax.optimization_barrier((pack, total))
+    following = shifted(pack_late, ("tm", "obs"), -1)
     any_spec = pl.BlockSpec(memory_space=pl.ANY)
-    plain = (*rows_args, tip_coupling, time_rhs, y, inv, total, tip_prior[None, :], tip_rhs[None, :], following)
-    block, low, tip, result, sol = call(
-        final_kernel,
-        [(2, B, B), (2, B, B), (2, K, B), (2, B), (1, K)],
+    plain = (*rows_args, tip_coupling, time_rhs, y, inv, total_late, tip_prior[None, :], tip_rhs[None, :])
+    low, part, tip, result, sol = call(
+        tip_kernel,
+        [(2, B, B), (B, B), (2, K, B), (2, B), (1, K)],
         [(T, 2 * T), (flat_rows, K)],
         grid=(1,),
-        in_specs=[whole(v.shape) for v in plain] + [any_spec, any_spec, whole((B, B))],
-        out_specs=[second, second, whole((2, K, B)), whole((2, B)), whole((1, K))],
-        aliases={len(plain): 1, len(plain) + 1: 0},
-    )(*plain, low, block, pack[:B])
+        in_specs=[whole(v.shape) for v in plain] + [whole((B, B)), any_spec],
+        out_specs=[second, whole((B, B)), whole((2, K, B)), whole((2, B)), whole((1, K))],
+        aliases={len(plain) + 1: 0},
+        cost=pl.CostEstimate(flops=10**9, bytes_accessed=40 * 10**6, transcendentals=0),
+    )(*plain, pack_late, low)
+    block, tip, result = call(
+        finish_kernel,
+        [(2, B, B), (2, K, B), (2, B)],
+        grid=(1,),
+        in_specs=[whole(wide), whole((B, B)), pl.BlockSpec((1, K, B), lambda i: (1, 0, 0)), whole((2, B)), any_spec],
+        out_specs=[second, pl.BlockSpec((1, K, B), lambda i: (1, 0, 0)), whole((2, B))],
+        aliases={2: 1, 4: 0},
+    )(following, part, tip, result, block)
     return block, low, tip, result, sol[0]
 
 

time: 93.5 us -> 82.3 us (0.88)
  Pallas kernels: 61.1 us -> 74.6 us
  blocking collectives: 7.61 us -> 0 us
  starting transfers between devices: 8.43 us -> 2.49 us
  waiting for transfers between devices: 5.7 us -> 0.01 us
  other arithmetic: 2.23 us -> 0 us
  local copies, waits for them, and re-layouts: 6.06 us -> 4.2 us
    pallas_call x1 -> x4, Pallas kernels: 14.6 us -> 32.1 us  [the longest x1 13.9 us: local(): call(route_kernel, [(count, B), (count, 128)], [(groups, CAP, width), (me...]
    all_gather x1 -> x0, blocking collectives: 7.61 us -> none  [local(): gathered = lax.all_gather(arrived, 'obs', axis=0, tiled=True)]
    all_to_all x1 -> x0, starting transfers between devices: 6.37 us -> none  [local(): lax.all_to_all(outgoing, 'tm', split_axis=0, concat_axis=0, tiled=True)]
    all_to_all x1 -> x0, waiting for transfers between devices: 5.69 us -> none  [local(): lax.all_to_all(outgoing, 'tm', split_axis=0, concat_axis=0, tiled=True)]
    unnamed x2 -> x4, local copies, waits for them, and re-layouts: 0.89 us -> 3.54 us
    pallas_call x1, Pallas kernels: 18.7 us -> 16.4 us  [local(): call(reduce_kernel, [(n, chunk, K)], [(n, chunk, K), (chunk, K), (n, chun...]
    slice x4 -> x0, local copies, waits for them, and re-layouts: 2.05 us -> none  [the longest x1 1.92 us: local(): pack[:B]]
    pallas_call x1, Pallas kernels: 27.8 us -> 26.1 us  [local(): call(local_kernel, [(2, B, B), (2, B, B), wide, (B, B), (n, chunk, K), wi...]
  transfers between devices with their start and end apart: 2 -> 1, of which waited for: 1 -> 0; matrix products, arithmetic and copies ran while one was open for 2% -> 0% of each run, Pallas kernels for 20% -> 15%
where the time goes in v3:
time: 82.3 us; the launch traced here: 81.9 us
  Pallas kernels  74.6 us (91%)
  local copies, waits for them, and re-layouts  4.2 us (5%)
  starting transfers between devices  2.49 us (3%)
    pallas_call x1, Pallas kernels, local(): call(local_kernel, [(2, B, B), (2, B, B), wide, (B, B), (n, chunk, K), wi...  26.1 us
    pallas_call x1, Pallas kernels, local(): call(reduce_kernel, [(n, chunk, K)], [(n, chunk, K), (chunk, K), (n, chun...  16.4 us
    pallas_call x1, Pallas kernels, local(): call(route_kernel, [(count, B), (count, 128)], [(groups, CAP, width), (me...  13.9 us
    pallas_call x1, Pallas kernels, local(): call(tip_kernel, [(2, B, B), (B, B), (2, K, B), (2, B), (1, K)], [(T, 2 *...  12.4 us
    pallas_call x1, Pallas kernels, local(): call(finish_kernel, [(2, B, B), (2, K, B), (2, B)], grid=(1,), in_specs=[...  3.75 us
    unnamed x4, local copies, waits for them, and re-layouts  3.54 us
    ppermute x1, starting transfers between devices, shifted(): lax.ppermute(value, axis, [(source, source + steps) for source in range(f...  2.49 us
    pallas_call x1, Pallas kernels, local(): call(pack_kernel, [(groups, CAP, width)])(obs_rows, obs_owner, obs_member)  2.01 us
  transfers between devices with their start and end apart: 1, of which 0 were waited for; matrix products, arithmetic and copies ran while one was open for 0% of the time, Pallas kernels for 15%

profile of v3, /device:TPU:1, one launch (start us, length us, event | category | flops | bytes accessed | tf_op | source)
XLA Modules:
  0.0 81.9 jit_solution(4615401736456613824)
XLA Ops:
  0.6 1.3 %copy.17.owner_ref = s32[8,1]{1,0:T(8,128)} copy(s32[8,1]{0,1:T(1,128)} %param.10) | data formatting | bytes 64 | tf_op args[1]
  2.0 1.3 %copy.18.member_ref = s32[8,1]{1,0:T(8,128)} copy(s32[8,1]{0,1:T(1,128)} %param.11) | data formatting | bytes 64 | tf_op args[2]
  3.3 2.0 %shard_map.128.x_ref = f32[8,2,896]{2,1,0:T(2,128)} custom-call(f32[8,768]{1,0:T(8,128)} %rows_ref.1, s32[8,1]{1,0:T(8,128)} %copy.17.owner_ref, s32[8,1]{1,0:T(8,128)} %copy.18.member_ref), custom_call_target="tpu_custom_call" | custom-call | tf_op jit(solution)/shard_map/pallas_call | solution.py:341
  5.3 13.9 %shard_map.129 = (f32[128,384]{1,0:T(8,128)}, f32[128,128]{1,0:T(8,128)}) custom-call(f32[8,2,896]{2,1,0:T(2,128)} %shard_map.128.x_ref), custom_call_target="tpu_custom_call" | custom-call | tf_op jit(solution)/shard_map/pallas_call | solution.py:343
  19.2 0.7 concatenate.6.label_ref
  19.9 26.1 %shard_map.130 = (f32[2,384,384]{2,1,0:T(8,128)}, f32[2,384,384]{2,1,0:T(8,128)}, f32[520,384]{1,0:T(8,128)}, f32[384,384]{1,0:T(8,128)}, f32[32,5,128]{2,1,0:T(8,128)}, /*index=5*/f32[520,384]{1,0:T(8,128)}) custom-call(f32[128,384]{1,0:T(8,128)} %get-tuple-element.23.rows_ref, f32[128,128]{1,0:T(8,128)} %get-tuple-element.24.tag_ref, ...), custom_call_target="tpu_custom_call" | custom-call | tf_op jit(solution)/shard_map/pallas_call | solution.py:371
  46.0 16.4 %shard_map.131.sum_ref = f32[32,5,128]{2,1,0:T(8,128)} custom-call(f32[32,5,128]{2,1,0:T(8,128)} %get-tuple-element.26.x_ref), custom_call_target="tpu_custom_call" | custom-call | tf_op jit(solution)/shard_map/pallas_call | solution.py:379
  62.4 2.5 %collective-permute-start = (f32[520,384]{1,0:T(8,128)}, f32[520,384]{1,0:T(8,128)S(1)}, u32[]{:S(2)}, u32[]{:S(2)}) collective-permute-start(f32[520,384]{1,0:T(8,128)} %get-tuple-element.27.fill_ref), channel_id=1, source_target_pairs={{1,0},{2,1},{3,2},{4,3},{5,4},{6,5},{7,6},{8,7},{9,8},{10,9},{11,1... | collective-permute-start | bytes 2396168 | tf_op jit(solution)/shard_map/ppermute | solution.py:328
  64.9 12.4 %shard_map.132 = (f32[2,384,384]{2,1,0:T(8,128)}, f32[384,384]{1,0:T(8,128)}, f32[2,128,384]{2,1,0:T(8,128)}, f32[2,384]{1,0:T(2,128)}, f32[1,128]{1,0:T(1,128)}) custom-call(f32[128,384]{1,0:T(8,128)} %get-tuple-element.23.rows_ref, f32[128,128]{1,0:T(8,128)} %get-tuple-element.24.tag_ref, ...), custom_call_target="tpu_custom_call", output_to_operand_aliasing={{0}: (12, {})} | custom-call | flops 1000000000 | bytes 40000000 | tf_op jit(solution)/shard_map/pallas_call | solution.py:393
  77.3 0.0 collective-permute-done.next_ref
  77.3 0.0 copy-start
  77.3 0.9 %copy-done = f32[520,384]{1,0:T(8,128)} copy-done((f32[520,384]{1,0:T(8,128)}, f32[520,384]{1,0:T(8,128)S(1)}, u32[]{:S(2)}) %copy-start) | copy-done | bytes 798744
  78.2 3.7 %shard_map.133 = (f32[2,384,384]{2,1,0:T(8,128)}, f32[2,128,384]{2,1,0:T(8,128)}, f32[2,384]{1,0:T(2,128)}) custom-call(f32[520,384]{1,0:T(8,128)} %copy-done, f32[384,384]{1,0:T(8,128)} %get-tuple-element.32.part_ref, f32[2,128,384]{2,1,0:T(8,128)} %get-tuple-element.33.tip_in, ...), custom_call_target="tpu_custom_call", output_to_operand_aliasing={{1}: (2, {}), {0}: (4, {})} | custom-call | tf_op jit(solution)/shard_map/pallas_call | solution.py:403
  (1 shorter events, 0.0 us)
Async XLA Ops:
  62.4 14.9 %collective-permute-start = (f32[520,384]{1,0:T(8,128)}, f32[520,384]{1,0:T(8,128)S(1)}, u32[]{:S(2)}, u32[]{:S(2)}) collective-permute-start(f32[520,384]{1,0:T(8,128)} %get-tuple-element.27.fill_ref), channel_id=1, source_target_pairs={{1,0},{2,1},{3,2},{4,3},{5,4},{6,5},{7,6},{8,7},{9,8},{10,9},{11,1... | collective-permute-start | bytes 2396168 | tf_op jit(solution)/shard_map/ppermute | solution.py:328
  77.3 0.9 %copy-start = (f32[520,384]{1,0:T(8,128)}, f32[520,384]{1,0:T(8,128)S(1)}, u32[]{:S(2)}) copy-start(f32[520,384]{1,0:T(8,128)S(1)} %collective-permute-done.next_ref) | copy-start | bytes 2396164

commit v4 on v3

--- a/solution.py
+++ b/solution.py
@@ -81,14 +81,14 @@
 
 
 def local_kernel(
-    rows_ref, tag_ref, label_ref, prior_ref, lower_ref, tip_ref, rhs_ref,
+    rows_ref, tag_ref, prior_ref, lower_ref, tip_ref, rhs_ref,
     factor_ref, low_ref, y_ref, inv_ref, terms_ref, pack_ref,
     gram, work, flat,
 ):
     B = prior_ref.shape[1]
     K = tip_ref.shape[1]
     nb = B // T
-    even = label_ref[0:1, 0:1]
+    even = (2 * lax.axis_index("obs") + 1).astype(jnp.float32)
     chosen = jnp.where(tag_ref[:, :1] == even, rows_ref[...], 0.0)
     gram[...] = dot_tn(chosen, chosen) + prior_ref[0:1, :] * eye(B)
     inv_ref[...] = jnp.zeros((B, B), jnp.float32)
@@ -109,7 +109,8 @@
             gram[hi:, hi:] = gram[hi:, hi:] - dot_tn(upper_rest, upper_rest)
             factor_ref[0, hi:, lo:hi] = upper_rest.T
     linv = inv_ref[...]
-    low = jnp.where(label_ref[1:2, 0:1] == 0.0, 0.0, lower_ref[0])
+    position = lax.axis_index("tm") * lax.axis_size("obs") + lax.axis_index("obs")
+    low = jnp.where(position == 0, 0.0, lower_ref[0])
     fill = dot_nn(linv, low)
     low_ref[0] = fill
     pack_ref[:B, :] = fill
@@ -185,7 +186,7 @@
 
 
 def tip_kernel(
-    rows_ref, tag_ref, label_ref, prior_ref, tip_ref, rhs_ref, y_ref, inv_ref, sum_ref,
+    rows_ref, tag_ref, prior_ref, tip_ref, rhs_ref, y_ref, inv_ref, sum_ref,
     tprior_ref, crhs_ref, fill_ref, low_in,
     low_ref, blk_ref, otip_ref, res_ref, sol_ref,
     work, flat,
@@ -200,7 +201,8 @@
     work[:, T:] = eye(T)
     xt = y_ref[:B, :]
     back = dot_nt(y_ref[...], xt)
-    chosen = jnp.where(tag_ref[:, :1] == label_ref[0:1, 0:1] + 1.0, rows_ref[...], 0.0)
+    odd = (2 * lax.axis_index("obs") + 2).astype(jnp.float32)
+    chosen = jnp.where(tag_ref[:, :1] == odd, rows_ref[...], 0.0)
     blk_ref[...] = dot_tn(chosen, chosen) + prior_ref[1:2, :] * eye(B) - back[:B]
     side = y_ref[B : B + K, :]
     otip_ref[0] = side
@@ -231,17 +233,17 @@
     groups = out_ref.shape[0]
     blocks, width = rows_ref.shape
     owners = owner_ref[...]
-    named = (lax.broadcasted_iota(jnp.int32, (blocks, groups), 1) == owners).astype(jnp.float32)
-    before = lax.broadcasted_iota(jnp.int32, (blocks, blocks), 1) < lax.broadcasted_iota(
-        jnp.int32, (blocks, blocks), 0
+    named = (lax.broadcasted_iota(jnp.int32, (groups, blocks), 0) == owners).astype(jnp.float32)
+    before = lax.broadcasted_iota(jnp.int32, (blocks, blocks), 0) < lax.broadcasted_iota(
+        jnp.int32, (blocks, blocks), 1
     )
-    rank = jnp.sum(dot_nn(before.astype(jnp.float32), named) * named, axis=1, keepdims=True)
+    rank = jnp.sum(dot_nn(named, before.astype(jnp.float32)) * named, axis=0, keepdims=True)
     slot = owners.astype(jnp.float32) * CAP + rank
-    spots = lax.broadcasted_iota(jnp.int32, (blocks, groups * CAP), 1).astype(jnp.float32)
+    spots = lax.broadcasted_iota(jnp.int32, (groups * CAP, blocks), 0).astype(jnp.float32)
     pick = (spots == slot).astype(jnp.float32)
-    tag = jnp.broadcast_to(member_ref[...].astype(jnp.float32) + 1.0, (blocks, 128))
-    rows = dot_tn(pick, rows_ref[...])
-    tags = dot_tn(pick, tag)
+    rows = dot_nn(pick, rows_ref[...])
+    tag = jnp.sum(pick * (member_ref[...].astype(jnp.float32) + 1.0), axis=1, keepdims=True)
+    tags = jnp.broadcast_to(tag, (groups * CAP, 128))
     for g in range(groups):
         out_ref[g, :, :width] = rows[g * CAP : (g + 1) * CAP, :]
         out_ref[g, :, width:] = tags[g * CAP : (g + 1) * CAP, :]
@@ -332,13 +334,11 @@
     obs_rows, obs_owner, obs_member, prior_diag, lower_coupling, tip_coupling, time_rhs, tip_prior, tip_rhs,
 ):
     groups = lax.axis_size("tm")
-    position = lax.axis_index(("tm", "obs"))
-    member_index = lax.axis_index("obs")
     B = prior_diag.shape[1]
     K = tip_coupling.shape[1]
     members = lax.axis_size("obs")
     width = R * B + 128
-    outgoing = call(pack_kernel, [(groups, CAP, width)])(obs_rows, obs_owner, obs_member)[0]
+    outgoing = call(pack_kernel, [(groups, CAP, width)])(obs_rows, obs_owner.reshape(1, -1), obs_member.reshape(1, -1))[0]
     count = members * groups * CAP * R
     rows_part, tags = call(
         route_kernel,
@@ -350,12 +350,6 @@
         collective_id=2,
         has_side_effects=True,
     )(outgoing)
-    label = jnp.concatenate(
-        [
-            jnp.full((1, 128), 2 * member_index + 1, jnp.float32),
-            jnp.full((7, 128), position, jnp.float32),
-        ]
-    )
     n = groups * lax.axis_size("obs")
     chunk = -(-(K + 1) // n)
     used = -(-(n * chunk + 8) // 8) * 8
@@ -366,7 +360,7 @@
     def whole(shape):
         return pl.BlockSpec(shape, lambda i: (0,) * len(shape))
 
-    rows_args = (rows_part, tags, label, prior_diag)
+    rows_args = (rows_part, tags, prior_diag)
     wide = (B + K + 8, B)
     block, low, y, inv, terms, pack = call(
         local_kernel,

time: 82.3 us -> 78.6 us (0.955)
  local copies, waits for them, and re-layouts: 4.2 us -> 0.89 us
    unnamed x4 -> x2, local copies, waits for them, and re-layouts: 3.54 us -> 0.89 us
  transfers between devices with their start and end apart: 1 -> 1, of which waited for: 0 -> 0; matrix products, arithmetic and copies ran while one was open for 0% -> 0% of each run, Pallas kernels for 15% -> 16%
where the time goes in v4:
time: 78.6 us; the launch traced here: 78.2 us
  Pallas kernels  74.2 us (94%)
  starting transfers between devices  2.49 us (3%)
  local copies, waits for them, and re-layouts  0.89 us (1%)
    pallas_call x1, Pallas kernels, local(): call(local_kernel, [(2, B, B), (2, B, B), wide, (B, B), (n, chunk, K), wi...  26 us
    pallas_call x1, Pallas kernels, local(): call(reduce_kernel, [(n, chunk, K)], [(n, chunk, K), (chunk, K), (n, chun...  16.4 us
    pallas_call x1, Pallas kernels, local(): call(route_kernel, [(count, B), (count, 128)], [(groups, CAP, width), (me...  13.9 us
    pallas_call x1, Pallas kernels, local(): call(tip_kernel, [(2, B, B), (B, B), (2, K, B), (2, B), (1, K)], [(T, 2 *...  12.4 us
    pallas_call x1, Pallas kernels, local(): call(finish_kernel, [(2, B, B), (2, K, B), (2, B)], grid=(1,), in_specs=[...  3.75 us
    ppermute x1, starting transfers between devices, shifted(): lax.ppermute(value, axis, [(source, source + steps) for source in range(f...  2.49 us
    pallas_call x1, Pallas kernels, local(): call(pack_kernel, [(groups, CAP, width)])  1.72 us
  transfers between devices with their start and end apart: 1, of which 0 were waited for; matrix products, arithmetic and copies ran while one was open for 0% of the time, Pallas kernels for 16%

profile of v4, /device:TPU:1, one launch (start us, length us, event | category | flops | bytes accessed | tf_op | source)
XLA Modules:
  0.0 78.2 jit_solution(2360856720915703470)
XLA Ops:
  0.6 1.7 %shard_map.128.x_ref = f32[8,2,896]{2,1,0:T(2,128)} custom-call(f32[8,768]{1,0:T(8,128)} %rows_ref.1, s32[1,8]{1,0:T(1,128)} %bitcast.7, s32[1,8]{1,0:T(1,128)} %bitcast.8), custom_call_target="tpu_custom_call" | custom-call | tf_op jit(solution)/shard_map/pallas_call | solution.py:341
  2.4 13.9 %shard_map.129 = (f32[128,384]{1,0:T(8,128)}, f32[128,128]{1,0:T(8,128)}) custom-call(f32[8,2,896]{2,1,0:T(2,128)} %shard_map.128.x_ref), custom_call_target="tpu_custom_call" | custom-call | tf_op jit(solution)/shard_map/pallas_call | solution.py:343
  16.2 26.0 %shard_map.130 = (f32[2,384,384]{2,1,0:T(8,128)}, f32[2,384,384]{2,1,0:T(8,128)}, f32[520,384]{1,0:T(8,128)}, f32[384,384]{1,0:T(8,128)}, f32[32,5,128]{2,1,0:T(8,128)}, /*index=5*/f32[520,384]{1,0:T(8,128)}) custom-call(f32[128,384]{1,0:T(8,128)} %get-tuple-element.23.rows_ref, f32[128,128]{1,0:T(8,128)} %get-tuple-element.24.tag_ref, f32[2,384]{1,0:T(2,128)} %prior_ref.3, ...), custom_call_target="tpu_custom_call" | custom-call | tf_op jit(solution)/shard_map/pallas_call | solution.py:365
  42.3 16.4 %shard_map.131.sum_ref = f32[32,5,128]{2,1,0:T(8,128)} custom-call(f32[32,5,128]{2,1,0:T(8,128)} %get-tuple-element.26.x_ref), custom_call_target="tpu_custom_call" | custom-call | tf_op jit(solution)/shard_map/pallas_call | solution.py:373
  58.7 2.5 %collective-permute-start = (f32[520,384]{1,0:T(8,128)}, f32[520,384]{1,0:T(8,128)S(1)}, u32[]{:S(2)}, u32[]{:S(2)}) collective-permute-start(f32[520,384]{1,0:T(8,128)} %get-tuple-element.27.fill_ref), channel_id=1, source_target_pairs={{1,0},{2,1},{3,2},{4,3},{5,4},{6,5},{7,6},{8,7},{9,8},{10,9},{11,1... | collective-permute-start | bytes 2396168 | tf_op jit(solution)/shard_map/ppermute | solution.py:330
  61.2 12.4 %shard_map.132 = (f32[2,384,384]{2,1,0:T(8,128)}, f32[384,384]{1,0:T(8,128)}, f32[2,128,384]{2,1,0:T(8,128)}, f32[2,384]{1,0:T(2,128)}, f32[1,128]{1,0:T(1,128)}) custom-call(f32[128,384]{1,0:T(8,128)} %get-tuple-element.23.rows_ref, f32[128,128]{1,0:T(8,128)} %get-tuple-element.24.tag_ref, f32[2,384]{1,0:T(2,128)} %prior_ref.3, ...), custom_call_target="tpu_custom_call", output_to_operand_aliasing={{0}: (11, {})} | custom-call | flops 1000000000 | bytes 40000000 | tf_op jit(solution)/shard_map/pallas_call | solution.py:387
  73.6 0.0 collective-permute-done.next_ref
  73.6 0.0 copy-start
  73.6 0.9 %copy-done = f32[520,384]{1,0:T(8,128)} copy-done((f32[520,384]{1,0:T(8,128)}, f32[520,384]{1,0:T(8,128)S(1)}, u32[]{:S(2)}) %copy-start) | copy-done | bytes 798744
  74.5 3.7 %shard_map.133 = (f32[2,384,384]{2,1,0:T(8,128)}, f32[2,128,384]{2,1,0:T(8,128)}, f32[2,384]{1,0:T(2,128)}) custom-call(f32[520,384]{1,0:T(8,128)} %copy-done, f32[384,384]{1,0:T(8,128)} %get-tuple-element.32.part_ref, f32[2,128,384]{2,1,0:T(8,128)} %get-tuple-element.33.tip_in, ...), custom_call_target="tpu_custom_call", output_to_operand_aliasing={{1}: (2, {}), {0}: (4, {})} | custom-call | tf_op jit(solution)/shard_map/pallas_call | solution.py:397
Async XLA Ops:
  58.7 14.9 %collective-permute-start = (f32[520,384]{1,0:T(8,128)}, f32[520,384]{1,0:T(8,128)S(1)}, u32[]{:S(2)}, u32[]{:S(2)}) collective-permute-start(f32[520,384]{1,0:T(8,128)} %get-tuple-element.27.fill_ref), channel_id=1, source_target_pairs={{1,0},{2,1},{3,2},{4,3},{5,4},{6,5},{7,6},{8,7},{9,8},{10,9},{11,1... | collective-permute-start | bytes 2396168 | tf_op jit(solution)/shard_map/ppermute | solution.py:330
  73.6 0.9 %copy-start = (f32[520,384]{1,0:T(8,128)}, f32[520,384]{1,0:T(8,128)S(1)}, u32[]{:S(2)}) copy-start(f32[520,384]{1,0:T(8,128)S(1)} %collective-permute-done.next_ref) | copy-start | bytes 2396164
